TPU v7x, 32 devices: a whole 2x2x4 slice. The times are simulated.
32 devices in a mesh: grp: 2 (over y), tile: 4 (over z), sub: 4 (over x, core).
Axes of the slice: x: 2, y: 2, z: 4, core: 2. Of those that a mesh axis runs over, the one named last changes fastest.
Arguments:
- features: bfloat16 [24, 32, 1024], P(('grp', 'tile'), 'sub'), parts along dimension 0, may hold values from -6 to 6
- out_grad: bfloat16 [24, 32, 1024], P(('grp', 'tile'), 'sub'), parts along dimension 0, may hold values from -6 to 6
- filters: bfloat16 [5, 32, 32], replicated, may hold values from -0.5 to 0.5
- tile_map: int32 [12], replicated, may hold values from 0 to 11, as said below
Outputs:
- in_grad: bfloat16 [24, 32, 1024], P(('grp', 'tile'), 'sub'), parts along dimension 0
- weight_grad: float32 [10, 32, 32], P('grp', 'sub'), parts along dimension 0
There are 2 independent parts, one for each index of `grp`. A program takes and returns all parts, laid end to end along the dimension named above; an argument that names none is the same for every part. Nothing has to cross between parts.
Inputs may be any that keep to these rules, and one draw needn't show every extreme that they name: tile_map[s] is the nested index of the tile held in slot s; slots 3 * j to 3 * j + 2 lie on index j of tile and hold the nested indices 3 * j to 3 * j + 2 in some order.
All inputs are finite; a program needn't handle non-finite values.
Results may differ from a plain program's by a relative error of at most 0.00045.
Values may be sent and summed in bfloat16 or wider, within the bound.
No kernel may reach another device: no remote copies, remote signals or barrier semaphores. Data moves between devices by JAX's collectives and lax.ppermute only.
A program may use at most 64 MiB of HBM per device.

v0:
```python
import math

import jax
import jax.numpy as jnp
import numpy as np
from jax import lax
from jax.sharding import PartitionSpec as P

K = 5


def from_behind(value, axis, steps):
    count = lax.axis_size(axis)
    pairs = [(source, (source + steps) % count) for source in range(count)]
    return lax.ppermute(value, axis, pairs)


def tile_coords(nested_code, bit_count):
    coord_x = nested_code * 0
    coord_y = nested_code * 0
    for bit_level in range(bit_count):
        coord_x = coord_x + nested_code // 4**bit_level % 2 * 2**bit_level
        coord_y = coord_y + nested_code // (2 * 4**bit_level) % 2 * 2**bit_level
    return (coord_x, coord_y)


def nested_index(coord_x, coord_y, bit_count):
    nested_code = coord_x * 0
    for bit_level in range(bit_count):
        nested_code = nested_code + coord_x // 2**bit_level % 2 * 4**bit_level
        nested_code = nested_code + coord_y // 2**bit_level % 2 * (2 * 4**bit_level)
    return nested_code


def pick(condition, when_true, when_false):
    return when_false + (when_true - when_false) * condition


def neighbour_codes(tile_ids, per_face, side_count):
    bit_count = side_count.bit_length() - 1
    face_id = tile_ids // per_face
    coord_x, coord_y = tile_coords(tile_ids % per_face, bit_count)
    column = face_id % 4
    is_north = face_id < 4
    is_south = face_id >= 8
    last_tile = side_count - 1

    def by_cycle(north_value, equator_value, south_value):
        return pick(is_north, north_value, pick(is_south, south_value, equator_value))

    side_rules = [
        (
            coord_x > 0,
            (face_id, coord_x - 1, coord_y, 1),
            (
                by_cycle(4 + column, 8 + (column + 3) % 4, 8 + (column + 3) % 4),
                by_cycle(last_tile, last_tile, coord_y),
                by_cycle(coord_y, coord_y, 0),
                by_cycle(1, 1, 2),
            ),
        ),
        (
            coord_x < last_tile,
            (face_id, coord_x + 1, coord_y, 0),
            (
                by_cycle((column + 1) % 4, column, 4 + (column + 1) % 4),
                by_cycle(coord_y, 0, 0),
                by_cycle(last_tile, coord_y, coord_y),
                by_cycle(3, 0, 0),
            ),
        ),
        (
            coord_y > 0,
            (face_id, coord_x, coord_y - 1, 3),
            (
                by_cycle(4 + (column + 1) % 4, 8 + column, 8 + (column + 1) % 4),
                by_cycle(coord_x, coord_x, 0),
                by_cycle(last_tile, last_tile, coord_x),
                by_cycle(3, 3, 0),
            ),
        ),
        (
            coord_y < last_tile,
            (face_id, coord_x, coord_y + 1, 2),
            (
                by_cycle((column + 3) % 4, (column + 3) % 4, 4 + column),
                by_cycle(last_tile, coord_x, coord_x),
                by_cycle(coord_x, 0, 0),
                by_cycle(1, 2, 2),
            ),
        ),
    ]
    target_list = []
    edge_list = []
    for inside, within, across in side_rules:
        chosen = [
            pick(inside, near_value, far_value) for near_value, far_value in zip(within, across)
        ]
        target_list.append(chosen[0] * per_face + nested_index(chosen[1], chosen[2], bit_count))
        edge_list.append(chosen[3] + tile_ids * 0)
    return (target_list, edge_list)


def neighbour_table(tile_map, per_face, side_count):
    target_list, edge_list = neighbour_codes(tile_map, per_face, side_count)
    targets = jnp.stack(target_list, axis=1).astype(jnp.int32)
    edges = jnp.stack(edge_list, axis=1).astype(jnp.int32)
    slot_of = jnp.argsort(tile_map).astype(jnp.int32)
    return (slot_of[targets].astype(jnp.int32), edges)


def peer_offsets(slot_count, device_count, per_face, side_count):
    tile_ids = np.arange(slot_count * device_count, dtype=np.int64)
    target_list, edge_list = neighbour_codes(tile_ids, per_face, side_count)
    targets = np.stack(target_list, axis=1)
    offsets = (tile_ids[:, None] // slot_count - targets // slot_count) % device_count
    distinct = sorted(set((int(value) for value in offsets.ravel())) - {0})
    position = np.zeros(device_count, dtype=np.int32)
    for order, value in enumerate(distinct):
        position[value] = order + 1
    return (distinct, position)


def edge_lines(values, tile_side):
    return jnp.stack(
        [
            values[..., :tile_side],
            values[..., -tile_side:],
            values[..., ::tile_side],
            values[..., tile_side - 1 :: tile_side],
        ],
        axis=1,
    )


def stencil(values, ghosts, tile_side):
    position = jnp.arange(values.shape[-1]) % tile_side
    zero_line = jnp.zeros_like(values[..., :1])
    upper_side = jnp.concatenate([ghosts[:, 0], values[..., :-tile_side]], axis=-1)
    lower_side = jnp.concatenate([values[..., tile_side:], ghosts[:, 1]], axis=-1)
    left_side = jnp.where(
        position == 0,
        jnp.repeat(ghosts[:, 2], tile_side, axis=-1),
        jnp.concatenate([zero_line, values[..., :-1]], axis=-1),
    )
    right_side = jnp.where(
        position == tile_side - 1,
        jnp.repeat(ghosts[:, 3], tile_side, axis=-1),
        jnp.concatenate([values[..., 1:], zero_line], axis=-1),
    )
    return -0.25 * (upper_side + lower_side + left_side + right_side)


def tile_total(filter_part):
    return lax.psum(filter_part, "tile")


def on_device(features, out_grad, filters, tile_map):
    slot_count = features.shape[0]
    group_channels = features.shape[1]
    tile_side = math.isqrt(features.shape[2])
    device_count = lax.axis_size("tile")
    total_tiles = slot_count * device_count
    side_count = math.isqrt(total_tiles // 12)
    scale_factor = 1.0 / math.sqrt(total_tiles * features.shape[2])
    highest = lax.Precision.HIGHEST
    slot_table, edge_table = neighbour_table(tile_map, total_tiles // 12, side_count)
    my_device = lax.axis_index("tile")
    first_slot = my_device * slot_count
    my_slots = lax.dynamic_slice_in_dim(slot_table, first_slot, slot_count, 0)
    my_edges = lax.dynamic_slice_in_dim(edge_table, first_slot, slot_count, 0)
    channel_start = lax.axis_index("sub") * group_channels
    weights = filters.astype(jnp.float32)
    distinct, position = peer_offsets(slot_count, device_count, total_tiles // 12, side_count)
    sender_gap = (my_device - my_slots // slot_count) % device_count
    local_rows = jnp.asarray(position)[sender_gap] * slot_count + my_slots % slot_count

    def laplace(values):
        border = edge_lines(values, tile_side).reshape(slot_count, 4, group_channels * tile_side)
        received = [border]
        for offset_value in distinct:
            received.append(from_behind(border, "tile", offset_value))
        stacked = jnp.concatenate(received, axis=0)
        stacked = stacked.reshape(stacked.shape[0], 4, group_channels, tile_side)
        ghosts = stacked[local_rows, my_edges]
        return stencil(values, ghosts, tile_side)

    whole_grad = lax.all_gather(out_grad, "sub", axis=1, tiled=True)
    cotangent = whole_grad.astype(jnp.float32)
    inputs = features.astype(jnp.float32)
    previous, current = (inputs, laplace(inputs))
    filter_terms = [
        jnp.einsum("sip,sop->io", inputs, cotangent, precision=highest),
        jnp.einsum("sip,sop->io", current, cotangent, precision=highest),
    ]
    for degree in range(2, K):
        previous, current = (current, 2.0 * laplace(current) - previous)
        filter_terms.append(jnp.einsum("sip,sop->io", current, cotangent, precision=highest))
    weight_grad = tile_total(jnp.stack(filter_terms)) * scale_factor
    row_block = lax.dynamic_slice_in_dim(weights, channel_start, group_channels, 1)

    def mixed(degree):
        return jnp.einsum("sop,io->sip", cotangent, row_block[degree], precision=highest)

    next_sum = mixed(K - 1)
    after_next = jnp.zeros_like(next_sum)
    for degree in range(K - 2, 0, -1):
        next_sum, after_next = (mixed(degree) + 2.0 * laplace(next_sum) - after_next, next_sum)
    in_grad = (mixed(0) + laplace(next_sum) - after_next).astype(jnp.bfloat16)
    return (in_grad, weight_grad)


def solution(mesh):
    placed = (P(("grp", "tile"), "sub", None), P(("grp", "tile"), "sub", None), P(), P())
    return jax.shard_map(
        on_device,
        mesh=mesh,
        in_specs=placed,
        out_specs=(P(("grp", "tile"), "sub", None), P("grp", "sub", None)),
        check_vma=False,
    )
```

profile of v0, /device:TPU:0, one launch (start us, length us, event | category | flops | bytes accessed | tf_op | source)
XLA Modules:
  0.0 89.9 jit_solution(3915343842741492382)
XLA Ops:
  0.7 0.8 fusion.100
  2.1 3.1 %collective-permute-start.12 = (f32[3,4,256]{2,0,1:T(4,128)S(1)}, f32[3,4,256]{2,0,1:T(4,128)S(1)}, u32[]{:S(2)}, u32[]{:S(2)}) collective-permute-start(f32[3,4,256]{2,0,1:T(4,128)S(1)} %constant_dynamic-update-slice_fusion.16), channel_id=1, source_target_pairs={{0,4},{4,8},{8,12},{12,0},{1,5},{5,9},{9,13},{13,1},{2,6},{6,10},{... | collective-permute-start | bytes 36872 | tf_op jit(solution)/shard_map/ppermute | solution.py:15
  5.2 2.6 %collective-permute-start.13 = (f32[3,4,256]{2,0,1:T(4,128)S(1)}, f32[3,4,256]{2,0,1:T(4,128)S(1)}, u32[]{:S(2)}, u32[]{:S(2)}) collective-permute-start(f32[3,4,256]{2,0,1:T(4,128)S(1)} %constant_dynamic-update-slice_fusion.16), channel_id=1, source_target_pairs={{0,8},{4,12},{8,0},{12,4},{1,9},{5,13},{9,1},{13,5},{2,10},{6,14},... | collective-permute-start | bytes 36872 | tf_op jit(solution)/shard_map/ppermute | solution.py:15
  7.8 1.3 %collective-permute-start.14 = (f32[3,4,256]{2,0,1:T(4,128)S(1)}, f32[3,4,256]{2,0,1:T(4,128)S(1)}, u32[]{:S(2)}, u32[]{:S(2)}) collective-permute-start(f32[3,4,256]{2,0,1:T(4,128)S(1)} %constant_dynamic-update-slice_fusion.16), channel_id=1, source_target_pairs={{0,12},{4,0},{8,4},{12,8},{1,13},{5,1},{9,5},{13,9},{2,14},{6,2},{... | collective-permute-start | bytes 36872 | tf_op jit(solution)/shard_map/ppermute | solution.py:15
  9.2 5.6 %all_gather.3 = bf16[3,32,1024]{2,1,0:T(8,128)(2,1)S(1)} all-gather(bf16[3,8,1024]{2,1,0:T(8,128)(2,1)S(1)} %copy-done.2), channel_id=1, replica_groups=mesh['grp'=2,'tile'=4,'sub'=4] {'sub'}, dimensions={1}, use_global_device_ids=true | all-gather | bytes 245760 | tf_op jit(solution)/shard_map/all_gather | solution.py:188
  15.7 0.7 collective-permute-start
  16.4 0.3 collective-permute-start.1
  17.3 0.6 copy-done.3
  18.3 1.2 %sort.17 = (s32[12]{0:T(128)}, s32[12]{0:T(128)S(1)}) sort(s32[12]{0:T(128)S(1)} %copy-done.3, s32[12]{0:T(128)S(1)} %iota.45), dimensions={0}, to_apply=%region_0.1 | sort | flops 48 | bytes 192 | tf_op jit(solution)/shard_map/jit(argsort)/sort | solution.py:108
  19.6 0.8 gather_fusion
  20.5 0.7 gather_fusion.1
  21.4 2.8 %collective-permute-start.2 = (f32[3,4,256]{2,0,1:T(4,128)S(1)}, f32[3,4,256]{2,0,1:T(4,128)S(1)}, u32[]{:S(2)}, u32[]{:S(2)}) collective-permute-start(f32[3,4,256]{2,0,1:T(4,128)S(1)} %constant_dynamic-update-slice_fusion), channel_id=1, source_target_pairs={{0,12},{4,0},{8,4},{12,8},{1,13},{5,1},{9,5},{13,9},{2,14},{6,2},{... | collective-permute-start | bytes 36872 | tf_op jit(solution)/shard_map/ppermute | solution.py:15
  24.4 0.6 gather_fusion.6
  25.2 0.2 reshape.322
  25.6 0.2 reshape.323
  26.7 0.6 collective-permute-start.15
  27.3 1.5 %collective-permute-start.16 = (f32[3,4,256]{2,0,1:T(4,128)S(1)}, f32[3,4,256]{2,0,1:T(4,128)S(1)}, u32[]{:S(2)}, u32[]{:S(2)}) collective-permute-start(f32[3,4,256]{2,0,1:T(4,128)S(1)} %constant_dynamic-update-slice_fusion.20), channel_id=1, source_target_pairs={{0,8},{4,12},{8,0},{12,4},{1,9},{5,13},{9,1},{13,5},{2,10},{6,14},... | collective-permute-start | bytes 36872 | tf_op jit(solution)/shard_map/ppermute | solution.py:15
  29.0 2.9 %collective-permute-start.17 = (f32[3,4,256]{2,0,1:T(4,128)S(1)}, f32[3,4,256]{2,0,1:T(4,128)S(1)}, u32[]{:S(2)}, u32[]{:S(2)}) collective-permute-start(f32[3,4,256]{2,0,1:T(4,128)S(1)} %constant_dynamic-update-slice_fusion.20), channel_id=1, source_target_pairs={{0,12},{4,0},{8,4},{12,8},{1,13},{5,1},{9,5},{13,9},{2,14},{6,2},{... | collective-permute-start | bytes 36872 | tf_op jit(solution)/shard_map/ppermute | solution.py:15
  32.1 0.6 gather_fusion.2
  32.9 0.2 reshape.310
  34.4 1.0 %collective-permute-start.4 = (f32[3,4,256]{2,0,1:T(4,128)S(1)}, f32[3,4,256]{2,0,1:T(4,128)S(1)}, u32[]{:S(2)}, u32[]{:S(2)}) collective-permute-start(f32[3,4,256]{2,0,1:T(4,128)S(1)} %constant_dynamic-update-slice_fusion.4), channel_id=1, source_target_pairs={{0,8},{4,12},{8,0},{12,4},{1,9},{5,13},{9,1},{13,5},{2,10},{6,14},... | collective-permute-start | bytes 36872 | tf_op jit(solution)/shard_map/ppermute | solution.py:15
  35.5 0.3 fusion.11
  35.8 2.9 %collective-permute-start.5 = (f32[3,4,256]{2,0,1:T(4,128)S(1)}, f32[3,4,256]{2,0,1:T(4,128)S(1)}, u32[]{:S(2)}, u32[]{:S(2)}) collective-permute-start(f32[3,4,256]{2,0,1:T(4,128)S(1)} %constant_dynamic-update-slice_fusion.4), channel_id=1, source_target_pairs={{0,12},{4,0},{8,4},{12,8},{1,13},{5,1},{9,5},{13,9},{2,14},{6,2},{... | collective-permute-start | bytes 36872 | tf_op jit(solution)/shard_map/ppermute | solution.py:15
  38.9 0.6 gather_fusion.7
  39.7 0.2 reshape.325
  41.2 0.6 collective-permute-start.18
  41.8 1.5 %collective-permute-start.19 = (f32[3,4,256]{2,0,1:T(4,128)S(1)}, f32[3,4,256]{2,0,1:T(4,128)S(1)}, u32[]{:S(2)}, u32[]{:S(2)}) collective-permute-start(f32[3,4,256]{2,0,1:T(4,128)S(1)} %constant_dynamic-update-slice_fusion.24), channel_id=1, source_target_pairs={{0,8},{4,12},{8,0},{12,4},{1,9},{5,13},{9,1},{13,5},{2,10},{6,14},... | collective-permute-start | bytes 36872 | tf_op jit(solution)/shard_map/ppermute | solution.py:15
  43.5 2.9 %collective-permute-start.20 = (f32[3,4,256]{2,0,1:T(4,128)S(1)}, f32[3,4,256]{2,0,1:T(4,128)S(1)}, u32[]{:S(2)}, u32[]{:S(2)}) collective-permute-start(f32[3,4,256]{2,0,1:T(4,128)S(1)} %constant_dynamic-update-slice_fusion.24), channel_id=1, source_target_pairs={{0,12},{4,0},{8,4},{12,8},{1,13},{5,1},{9,5},{13,9},{2,14},{6,2},{... | collective-permute-start | bytes 36872 | tf_op jit(solution)/shard_map/ppermute | solution.py:15
  46.6 0.6 gather_fusion.3
  48.9 1.0 %collective-permute-start.7 = (f32[3,4,256]{2,0,1:T(4,128)S(1)}, f32[3,4,256]{2,0,1:T(4,128)S(1)}, u32[]{:S(2)}, u32[]{:S(2)}) collective-permute-start(f32[3,4,256]{2,0,1:T(4,128)S(1)} %constant_dynamic-update-slice_fusion.8), channel_id=1, source_target_pairs={{0,8},{4,12},{8,0},{12,4},{1,9},{5,13},{9,1},{13,5},{2,10},{6,14},... | collective-permute-start | bytes 36872 | tf_op jit(solution)/shard_map/ppermute | solution.py:15
  50.0 0.3 fusion.10
  50.3 2.9 %collective-permute-start.8 = (f32[3,4,256]{2,0,1:T(4,128)S(1)}, f32[3,4,256]{2,0,1:T(4,128)S(1)}, u32[]{:S(2)}, u32[]{:S(2)}) collective-permute-start(f32[3,4,256]{2,0,1:T(4,128)S(1)} %constant_dynamic-update-slice_fusion.8), channel_id=1, source_target_pairs={{0,12},{4,0},{8,4},{12,8},{1,13},{5,1},{9,5},{13,9},{2,14},{6,2},{... | collective-permute-start | bytes 36872 | tf_op jit(solution)/shard_map/ppermute | solution.py:15
  53.4 0.6 gather_fusion.8
  54.6 0.2 reshape.329
  55.7 0.6 collective-permute-start.21
  56.3 1.5 %collective-permute-start.22 = (f32[3,4,256]{2,0,1:T(4,128)S(1)}, f32[3,4,256]{2,0,1:T(4,128)S(1)}, u32[]{:S(2)}, u32[]{:S(2)}) collective-permute-start(f32[3,4,256]{2,0,1:T(4,128)S(1)} %constant_dynamic-update-slice_fusion.28), channel_id=1, source_target_pairs={{0,8},{4,12},{8,0},{12,4},{1,9},{5,13},{9,1},{13,5},{2,10},{6,14},... | collective-permute-start | bytes 36872 | tf_op jit(solution)/shard_map/ppermute | solution.py:15
  58.0 2.9 %collective-permute-start.23 = (f32[3,4,256]{2,0,1:T(4,128)S(1)}, f32[3,4,256]{2,0,1:T(4,128)S(1)}, u32[]{:S(2)}, u32[]{:S(2)}) collective-permute-start(f32[3,4,256]{2,0,1:T(4,128)S(1)} %constant_dynamic-update-slice_fusion.28), channel_id=1, source_target_pairs={{0,12},{4,0},{8,4},{12,8},{1,13},{5,1},{9,5},{13,9},{2,14},{6,2},{... | collective-permute-start | bytes 36872 | tf_op jit(solution)/shard_map/ppermute | solution.py:15
  61.1 0.6 gather_fusion.4
  63.3 1.0 %collective-permute-start.10 = (f32[3,4,256]{2,0,1:T(4,128)S(1)}, f32[3,4,256]{2,0,1:T(4,128)S(1)}, u32[]{:S(2)}, u32[]{:S(2)}) collective-permute-start(f32[3,4,256]{2,0,1:T(4,128)S(1)} %constant_dynamic-update-slice_fusion.12), channel_id=1, source_target_pairs={{0,8},{4,12},{8,0},{12,4},{1,9},{5,13},{9,1},{13,5},{2,10},{6,14},... | collective-permute-start | bytes 36872 | tf_op jit(solution)/shard_map/ppermute | solution.py:15
  64.3 0.9 %collective-permute-start.11 = (f32[3,4,256]{2,0,1:T(4,128)S(1)}, f32[3,4,256]{2,0,1:T(4,128)S(1)}, u32[]{:S(2)}, u32[]{:S(2)}) collective-permute-start(f32[3,4,256]{2,0,1:T(4,128)S(1)} %constant_dynamic-update-slice_fusion.12), channel_id=1, source_target_pairs={{0,12},{4,0},{8,4},{12,8},{1,13},{5,1},{9,5},{13,9},{2,14},{6,2},{... | collective-permute-start | bytes 36872 | tf_op jit(solution)/shard_map/ppermute | solution.py:15
  65.3 0.3 fusion.9
  65.7 1.1 %collective-permute-start.9 = (f32[3,4,256]{2,0,1:T(4,128)S(1)}, f32[3,4,256]{2,0,1:T(4,128)S(1)}, u32[]{:S(2)}, u32[]{:S(2)}) collective-permute-start(f32[3,4,256]{2,0,1:T(4,128)S(1)} %constant_dynamic-update-slice_fusion.12), channel_id=1, source_target_pairs={{0,4},{4,8},{8,12},{12,0},{1,5},{5,9},{9,13},{13,1},{2,6},{6,10},{... | collective-permute-start | bytes 36872 | tf_op jit(solution)/shard_map/ppermute | solution.py:15
  67.1 0.6 gather_fusion.9
  68.4 0.3 fusion.8
  68.7 18.3 %psum.7 = f32[5,8,32]{2,1,0:T(8,128)S(1)} all-reduce(f32[5,8,32]{2,1,0:T(8,128)S(1)} %fusion.8), channel_id=1, replica_groups=mesh['grp'=2,'tile'=4,'sub'=4] {'tile'}, use_global_device_ids=true, to_apply=%region_1.2 | all-reduce | flops 1280 | bytes 10240 | tf_op jit(solution)/shard_map/psum | solution.py:155
  87.0 0.6 broadcast_multiply_fusion
  87.8 0.6 gather_fusion.5
  89.2 0.8 fusion.7
  (223 shorter events, 15.4 us)
Async XLA Ops:
  0.6 14.1 %copy-start = (bf16[5,32,32]{2,1,0:T(8,128)(2,1)S(1)}, bf16[5,32,32]{2,1,0:T(8,128)(2,1)}, u32[]{:S(2)}) copy-start(bf16[5,32,32]{2,1,0:T(8,128)(2,1)} %param.7) | copy-start | bytes 30724
  0.6 0.8 copy-start.1
  1.8 7.4 %copy-start.2 = (bf16[3,8,1024]{2,1,0:T(8,128)(2,1)S(1)}, bf16[3,8,1024]{2,1,0:T(8,128)(2,1)}, u32[]{:S(2)}) copy-start(bf16[3,8,1024]{2,1,0:T(8,128)(2,1)} %param.6) | copy-start | bytes 147460
  2.1 19.3 %collective-permute-start.12 = (f32[3,4,256]{2,0,1:T(4,128)S(1)}, f32[3,4,256]{2,0,1:T(4,128)S(1)}, u32[]{:S(2)}, u32[]{:S(2)}) collective-permute-start(f32[3,4,256]{2,0,1:T(4,128)S(1)} %constant_dynamic-update-slice_fusion.16), channel_id=1, source_target_pairs={{0,4},{4,8},{8,12},{12,0},{1,5},{5,9},{9,13},{13,1},{2,6},{6,10},{... | collective-permute-start | bytes 36872 | tf_op jit(solution)/shard_map/ppermute | solution.py:15
  5.2 19.0 %collective-permute-start.13 = (f32[3,4,256]{2,0,1:T(4,128)S(1)}, f32[3,4,256]{2,0,1:T(4,128)S(1)}, u32[]{:S(2)}, u32[]{:S(2)}) collective-permute-start(f32[3,4,256]{2,0,1:T(4,128)S(1)} %constant_dynamic-update-slice_fusion.16), channel_id=1, source_target_pairs={{0,8},{4,12},{8,0},{12,4},{1,9},{5,13},{9,1},{13,5},{2,10},{6,14},... | collective-permute-start | bytes 36872 | tf_op jit(solution)/shard_map/ppermute | solution.py:15
  7.8 16.4 %collective-permute-start.14 = (f32[3,4,256]{2,0,1:T(4,128)S(1)}, f32[3,4,256]{2,0,1:T(4,128)S(1)}, u32[]{:S(2)}, u32[]{:S(2)}) collective-permute-start(f32[3,4,256]{2,0,1:T(4,128)S(1)} %constant_dynamic-update-slice_fusion.16), channel_id=1, source_target_pairs={{0,12},{4,0},{8,4},{12,8},{1,13},{5,1},{9,5},{13,9},{2,14},{6,2},{... | collective-permute-start | bytes 36872 | tf_op jit(solution)/shard_map/ppermute | solution.py:15
  15.7 13.3 %collective-permute-start = (f32[3,4,256]{2,0,1:T(4,128)S(1)}, f32[3,4,256]{2,0,1:T(4,128)S(1)}, u32[]{:S(2)}, u32[]{:S(2)}) collective-permute-start(f32[3,4,256]{2,0,1:T(4,128)S(1)} %constant_dynamic-update-slice_fusion), channel_id=1, source_target_pairs={{0,4},{4,8},{8,12},{12,0},{1,5},{5,9},{9,13},{13,1},{2,6},{6,10},{... | collective-permute-start | bytes 36872 | tf_op jit(solution)/shard_map/ppermute | solution.py:15
  16.4 15.5 %collective-permute-start.1 = (f32[3,4,256]{2,0,1:T(4,128)S(1)}, f32[3,4,256]{2,0,1:T(4,128)S(1)}, u32[]{:S(2)}, u32[]{:S(2)}) collective-permute-start(f32[3,4,256]{2,0,1:T(4,128)S(1)} %constant_dynamic-update-slice_fusion), channel_id=1, source_target_pairs={{0,8},{4,12},{8,0},{12,4},{1,9},{5,13},{9,1},{13,5},{2,10},{6,14},... | collective-permute-start | bytes 36872 | tf_op jit(solution)/shard_map/ppermute | solution.py:15
  17.2 0.7 copy-start.3
  21.4 10.5 %collective-permute-start.2 = (f32[3,4,256]{2,0,1:T(4,128)S(1)}, f32[3,4,256]{2,0,1:T(4,128)S(1)}, u32[]{:S(2)}, u32[]{:S(2)}) collective-permute-start(f32[3,4,256]{2,0,1:T(4,128)S(1)} %constant_dynamic-update-slice_fusion), channel_id=1, source_target_pairs={{0,12},{4,0},{8,4},{12,8},{1,13},{5,1},{9,5},{13,9},{2,14},{6,2},{... | collective-permute-start | bytes 36872 | tf_op jit(solution)/shard_map/ppermute | solution.py:15
  26.7 9.2 %collective-permute-start.15 = (f32[3,4,256]{2,0,1:T(4,128)S(1)}, f32[3,4,256]{2,0,1:T(4,128)S(1)}, u32[]{:S(2)}, u32[]{:S(2)}) collective-permute-start(f32[3,4,256]{2,0,1:T(4,128)S(1)} %constant_dynamic-update-slice_fusion.20), channel_id=1, source_target_pairs={{0,4},{4,8},{8,12},{12,0},{1,5},{5,9},{9,13},{13,1},{2,6},{6,10},{... | collective-permute-start | bytes 36872 | tf_op jit(solution)/shard_map/ppermute | solution.py:15
  27.3 11.4 %collective-permute-start.16 = (f32[3,4,256]{2,0,1:T(4,128)S(1)}, f32[3,4,256]{2,0,1:T(4,128)S(1)}, u32[]{:S(2)}, u32[]{:S(2)}) collective-permute-start(f32[3,4,256]{2,0,1:T(4,128)S(1)} %constant_dynamic-update-slice_fusion.20), channel_id=1, source_target_pairs={{0,8},{4,12},{8,0},{12,4},{1,9},{5,13},{9,1},{13,5},{2,10},{6,14},... | collective-permute-start | bytes 36872 | tf_op jit(solution)/shard_map/ppermute | solution.py:15
  29.0 9.7 %collective-permute-start.17 = (f32[3,4,256]{2,0,1:T(4,128)S(1)}, f32[3,4,256]{2,0,1:T(4,128)S(1)}, u32[]{:S(2)}, u32[]{:S(2)}) collective-permute-start(f32[3,4,256]{2,0,1:T(4,128)S(1)} %constant_dynamic-update-slice_fusion.20), channel_id=1, source_target_pairs={{0,12},{4,0},{8,4},{12,8},{1,13},{5,1},{9,5},{13,9},{2,14},{6,2},{... | collective-permute-start | bytes 36872 | tf_op jit(solution)/shard_map/ppermute | solution.py:15
  34.3 9.1 %collective-permute-start.3 = (f32[3,4,256]{2,0,1:T(4,128)S(1)}, f32[3,4,256]{2,0,1:T(4,128)S(1)}, u32[]{:S(2)}, u32[]{:S(2)}) collective-permute-start(f32[3,4,256]{2,0,1:T(4,128)S(1)} %constant_dynamic-update-slice_fusion.4), channel_id=1, source_target_pairs={{0,4},{4,8},{8,12},{12,0},{1,5},{5,9},{9,13},{13,1},{2,6},{6,10},{... | collective-permute-start | bytes 36872 | tf_op jit(solution)/shard_map/ppermute | solution.py:15
  34.4 12.0 %collective-permute-start.4 = (f32[3,4,256]{2,0,1:T(4,128)S(1)}, f32[3,4,256]{2,0,1:T(4,128)S(1)}, u32[]{:S(2)}, u32[]{:S(2)}) collective-permute-start(f32[3,4,256]{2,0,1:T(4,128)S(1)} %constant_dynamic-update-slice_fusion.4), channel_id=1, source_target_pairs={{0,8},{4,12},{8,0},{12,4},{1,9},{5,13},{9,1},{13,5},{2,10},{6,14},... | collective-permute-start | bytes 36872 | tf_op jit(solution)/shard_map/ppermute | solution.py:15
  35.8 10.6 %collective-permute-start.5 = (f32[3,4,256]{2,0,1:T(4,128)S(1)}, f32[3,4,256]{2,0,1:T(4,128)S(1)}, u32[]{:S(2)}, u32[]{:S(2)}) collective-permute-start(f32[3,4,256]{2,0,1:T(4,128)S(1)} %constant_dynamic-update-slice_fusion.4), channel_id=1, source_target_pairs={{0,12},{4,0},{8,4},{12,8},{1,13},{5,1},{9,5},{13,9},{2,14},{6,2},{... | collective-permute-start | bytes 36872 | tf_op jit(solution)/shard_map/ppermute | solution.py:15
  41.2 9.2 %collective-permute-start.18 = (f32[3,4,256]{2,0,1:T(4,128)S(1)}, f32[3,4,256]{2,0,1:T(4,128)S(1)}, u32[]{:S(2)}, u32[]{:S(2)}) collective-permute-start(f32[3,4,256]{2,0,1:T(4,128)S(1)} %constant_dynamic-update-slice_fusion.24), channel_id=1, source_target_pairs={{0,4},{4,8},{8,12},{12,0},{1,5},{5,9},{9,13},{13,1},{2,6},{6,10},{... | collective-permute-start | bytes 36872 | tf_op jit(solution)/shard_map/ppermute | solution.py:15
  41.8 11.4 %collective-permute-start.19 = (f32[3,4,256]{2,0,1:T(4,128)S(1)}, f32[3,4,256]{2,0,1:T(4,128)S(1)}, u32[]{:S(2)}, u32[]{:S(2)}) collective-permute-start(f32[3,4,256]{2,0,1:T(4,128)S(1)} %constant_dynamic-update-slice_fusion.24), channel_id=1, source_target_pairs={{0,8},{4,12},{8,0},{12,4},{1,9},{5,13},{9,1},{13,5},{2,10},{6,14},... | collective-permute-start | bytes 36872 | tf_op jit(solution)/shard_map/ppermute | solution.py:15
  43.5 9.7 %collective-permute-start.20 = (f32[3,4,256]{2,0,1:T(4,128)S(1)}, f32[3,4,256]{2,0,1:T(4,128)S(1)}, u32[]{:S(2)}, u32[]{:S(2)}) collective-permute-start(f32[3,4,256]{2,0,1:T(4,128)S(1)} %constant_dynamic-update-slice_fusion.24), channel_id=1, source_target_pairs={{0,12},{4,0},{8,4},{12,8},{1,13},{5,1},{9,5},{13,9},{2,14},{6,2},{... | collective-permute-start | bytes 36872 | tf_op jit(solution)/shard_map/ppermute | solution.py:15
  48.8 9.1 %collective-permute-start.6 = (f32[3,4,256]{2,0,1:T(4,128)S(1)}, f32[3,4,256]{2,0,1:T(4,128)S(1)}, u32[]{:S(2)}, u32[]{:S(2)}) collective-permute-start(f32[3,4,256]{2,0,1:T(4,128)S(1)} %constant_dynamic-update-slice_fusion.8), channel_id=1, source_target_pairs={{0,4},{4,8},{8,12},{12,0},{1,5},{5,9},{9,13},{13,1},{2,6},{6,10},{... | collective-permute-start | bytes 36872 | tf_op jit(solution)/shard_map/ppermute | solution.py:15
  48.9 12.0 %collective-permute-start.7 = (f32[3,4,256]{2,0,1:T(4,128)S(1)}, f32[3,4,256]{2,0,1:T(4,128)S(1)}, u32[]{:S(2)}, u32[]{:S(2)}) collective-permute-start(f32[3,4,256]{2,0,1:T(4,128)S(1)} %constant_dynamic-update-slice_fusion.8), channel_id=1, source_target_pairs={{0,8},{4,12},{8,0},{12,4},{1,9},{5,13},{9,1},{13,5},{2,10},{6,14},... | collective-permute-start | bytes 36872 | tf_op jit(solution)/shard_map/ppermute | solution.py:15
  50.3 10.6 %collective-permute-start.8 = (f32[3,4,256]{2,0,1:T(4,128)S(1)}, f32[3,4,256]{2,0,1:T(4,128)S(1)}, u32[]{:S(2)}, u32[]{:S(2)}) collective-permute-start(f32[3,4,256]{2,0,1:T(4,128)S(1)} %constant_dynamic-update-slice_fusion.8), channel_id=1, source_target_pairs={{0,12},{4,0},{8,4},{12,8},{1,13},{5,1},{9,5},{13,9},{2,14},{6,2},{... | collective-permute-start | bytes 36872 | tf_op jit(solution)/shard_map/ppermute | solution.py:15
  55.7 10.0 %collective-permute-start.21 = (f32[3,4,256]{2,0,1:T(4,128)S(1)}, f32[3,4,256]{2,0,1:T(4,128)S(1)}, u32[]{:S(2)}, u32[]{:S(2)}) collective-permute-start(f32[3,4,256]{2,0,1:T(4,128)S(1)} %constant_dynamic-update-slice_fusion.28), channel_id=1, source_target_pairs={{0,4},{4,8},{8,12},{12,0},{1,5},{5,9},{9,13},{13,1},{2,6},{6,10},{... | collective-permute-start | bytes 36872 | tf_op jit(solution)/shard_map/ppermute | solution.py:15
  56.3 10.6 %collective-permute-start.22 = (f32[3,4,256]{2,0,1:T(4,128)S(1)}, f32[3,4,256]{2,0,1:T(4,128)S(1)}, u32[]{:S(2)}, u32[]{:S(2)}) collective-permute-start(f32[3,4,256]{2,0,1:T(4,128)S(1)} %constant_dynamic-update-slice_fusion.28), channel_id=1, source_target_pairs={{0,8},{4,12},{8,0},{12,4},{1,9},{5,13},{9,1},{13,5},{2,10},{6,14},... | collective-permute-start | bytes 36872 | tf_op jit(solution)/shard_map/ppermute | solution.py:15
  58.0 8.9 %collective-permute-start.23 = (f32[3,4,256]{2,0,1:T(4,128)S(1)}, f32[3,4,256]{2,0,1:T(4,128)S(1)}, u32[]{:S(2)}, u32[]{:S(2)}) collective-permute-start(f32[3,4,256]{2,0,1:T(4,128)S(1)} %constant_dynamic-update-slice_fusion.28), channel_id=1, source_target_pairs={{0,12},{4,0},{8,4},{12,8},{1,13},{5,1},{9,5},{13,9},{2,14},{6,2},{... | collective-permute-start | bytes 36872 | tf_op jit(solution)/shard_map/ppermute | solution.py:15
  63.3 24.3 %collective-permute-start.10 = (f32[3,4,256]{2,0,1:T(4,128)S(1)}, f32[3,4,256]{2,0,1:T(4,128)S(1)}, u32[]{:S(2)}, u32[]{:S(2)}) collective-permute-start(f32[3,4,256]{2,0,1:T(4,128)S(1)} %constant_dynamic-update-slice_fusion.12), channel_id=1, source_target_pairs={{0,8},{4,12},{8,0},{12,4},{1,9},{5,13},{9,1},{13,5},{2,10},{6,14},... | collective-permute-start | bytes 36872 | tf_op jit(solution)/shard_map/ppermute | solution.py:15
  64.3 23.3 %collective-permute-start.11 = (f32[3,4,256]{2,0,1:T(4,128)S(1)}, f32[3,4,256]{2,0,1:T(4,128)S(1)}, u32[]{:S(2)}, u32[]{:S(2)}) collective-permute-start(f32[3,4,256]{2,0,1:T(4,128)S(1)} %constant_dynamic-update-slice_fusion.12), channel_id=1, source_target_pairs={{0,12},{4,0},{8,4},{12,8},{1,13},{5,1},{9,5},{13,9},{2,14},{6,2},{... | collective-permute-start | bytes 36872 | tf_op jit(solution)/shard_map/ppermute | solution.py:15
  65.7 21.9 %collective-permute-start.9 = (f32[3,4,256]{2,0,1:T(4,128)S(1)}, f32[3,4,256]{2,0,1:T(4,128)S(1)}, u32[]{:S(2)}, u32[]{:S(2)}) collective-permute-start(f32[3,4,256]{2,0,1:T(4,128)S(1)} %constant_dynamic-update-slice_fusion.12), channel_id=1, source_target_pairs={{0,4},{4,8},{8,12},{12,0},{1,5},{5,9},{9,13},{13,1},{2,6},{6,10},{... | collective-permute-start | bytes 36872 | tf_op jit(solution)/shard_map/ppermute | solution.py:15
where the time goes:
time: 90.1 us; the launch traced here: 89.9 us
  starting transfers between devices  36.9 us (41%)
  blocking collectives  23.9 us (27%)
  local copies, waits for them, and re-layouts  22.3 us (25%)
  matrix products  2.63 us (3%)
  other arithmetic  2.6 us (3%)
  between operations  1.55 us (2%)
    ppermute x24, starting transfers between devices, from_behind(): return lax.ppermute(value, axis, pairs)  36.9 us
    psum x1, blocking collectives, tile_total(): return lax.psum(filter_part, 'tile')  18.3 us
    all_gather x1, blocking collectives, on_device(): whole_grad = lax.all_gather(out_grad, 'sub', axis=1, tiled=True)  5.58 us
    gather x8, local copies, waits for them, and re-layouts, laplace(): ghosts = stacked[local_rows, my_edges]  4.87 us
    another operation x40, local copies, waits for them, and re-layouts, edge_lines(): jnp.stack([values[..., :tile_side], values[..., -tile_side:], values[...,...  2.57 us
  transfers between devices with their start and end apart: 24, of which 0 were waited for; matrix products, arithmetic and copies ran while one was open for 26% of the time, Pallas kernels for 0%

commit v1 on v0

--- a/solution.py
+++ b/solution.py
@@ -1,9 +1,12 @@
+import functools
 import math
 
 import jax
 import jax.numpy as jnp
 import numpy as np
 from jax import lax
+from jax.experimental import pallas as pl
+from jax.experimental.pallas import tpu as pltpu
 from jax.sharding import PartitionSpec as P
 
 K = 5
@@ -155,7 +158,7 @@
     return lax.psum(filter_part, "tile")
 
 
-def on_device(features, out_grad, filters, tile_map):
+def by_halos(features, out_grad, filters, tile_map):
     slot_count = features.shape[0]
     group_channels = features.shape[1]
     tile_side = math.isqrt(features.shape[2])
@@ -210,6 +213,298 @@
     return (in_grad, weight_grad)
 
 
+LANES = 128
+GATHER_LIMIT = 2 << 20
+
+
+def lane_gather(block, lane_index):
+    index = jnp.broadcast_to(lane_index, block.shape)
+    return jnp.take_along_axis(block, index, axis=1, mode="promise_in_bounds")
+
+
+class FaceStencil:
+    def __init__(self, tile_count, tile_side):
+        per_face = tile_count // 12
+        side_count = math.isqrt(per_face)
+        targets, edges = neighbour_codes(
+            np.arange(tile_count, dtype=np.int64), per_face, side_count
+        )
+        self.targets = np.stack(targets, axis=1)
+        self.edges = np.stack(edges, axis=1)
+        self.side = tile_side
+        self.rows = LANES // tile_side
+        self.blocks = tile_side * tile_side // LANES
+        self.lane = lax.broadcasted_iota(jnp.int32, (1, LANES), 1)
+
+    def block(self, ref, tile, number):
+        return ref[tile, :, number * LANES : (number + 1) * LANES]
+
+    def row_as_row(self, ref, tile, edge):
+        if edge == 0:
+            return self.block(ref, tile, 0)
+        return self.block(ref, tile, self.blocks - 1)
+
+    def column_as_row(self, ref, tile, edge, first_lane):
+        lane, side, rows = self.lane, self.side, self.rows
+        column = 0 if edge == 2 else side - 1
+        place = lane - first_lane
+        index = place % rows * side + column
+        index = jnp.where((place >= 0) & (place < side), index, 0)
+        line = lane_gather(self.block(ref, tile, 0), index)
+        for number in range(1, self.blocks):
+            moved = lane_gather(self.block(ref, tile, number), index)
+            line = jnp.where(place // rows == number, moved, line)
+        return line
+
+    def row_as_column(self, ref, tile, edge):
+        block = self.row_as_row(ref, tile, edge)
+        base = 0 if edge == 0 else LANES - self.side
+        return [
+            lane_gather(block, self.lane // self.side + (base + number * self.rows))
+            for number in range(self.blocks)
+        ]
+
+    def neighbour_sum(self, ref, tile):
+        lane, side, last = self.lane, self.side, self.blocks - 1
+        target, edge = self.targets[tile], self.edges[tile]
+        value = [self.block(ref, tile, number) for number in range(self.blocks)]
+
+        if edge[0] == 1:
+            above = self.row_as_row(ref, target[0], 1)
+        elif edge[0] == 0:
+            above = pltpu.roll(self.row_as_row(ref, target[0], 0), LANES - side, 1)
+        else:
+            above = self.column_as_row(ref, target[0], edge[0], LANES - side)
+        down_turn = [pltpu.roll(block, side, 1) for block in [above] + value]
+        upper = [
+            jnp.where(lane < side, down_turn[number], down_turn[number + 1])
+            for number in range(self.blocks)
+        ]
+        if edge[1] == 0:
+            below = self.row_as_row(ref, target[1], 0)
+        elif edge[1] == 1:
+            below = pltpu.roll(self.row_as_row(ref, target[1], 1), side, 1)
+        else:
+            below = self.column_as_row(ref, target[1], edge[1], 0)
+        up_turn = [pltpu.roll(block, LANES - side, 1) for block in value + [below]]
+        lower = [
+            jnp.where(lane >= LANES - side, up_turn[number + 1], up_turn[number])
+            for number in range(self.blocks)
+        ]
+        column = lane % side
+        row_start = lane - column
+        if edge[2] >= 2:
+            beside = [self.block(ref, target[2], number) for number in range(self.blocks)]
+            if edge[2] == 2:
+                turn = row_start + (column + 1) % side
+                beside = [lane_gather(block, turn) for block in beside]
+        else:
+            beside = self.row_as_column(ref, target[2], edge[2])
+        turn = row_start + (column + side - 1) % side
+        left = [
+            lane_gather(jnp.where(column == side - 1, ghost, block), turn)
+            for ghost, block in zip(beside, value)
+        ]
+        if edge[3] >= 2:
+            beside = [self.block(ref, target[3], number) for number in range(self.blocks)]
+            if edge[3] == 3:
+                turn = row_start + (column + side - 1) % side
+                beside = [lane_gather(block, turn) for block in beside]
+        else:
+            beside = self.row_as_column(ref, target[3], edge[3])
+        turn = row_start + (column + 1) % side
+        right = [
+            lane_gather(jnp.where(column == 0, ghost, block), turn)
+            for ghost, block in zip(beside, value)
+        ]
+        return [
+            (upper[number] + lower[number]) + (left[number] + right[number])
+            for number in range(self.blocks)
+        ]
+
+
+def split_rows(value):
+    high = value.astype(jnp.bfloat16).astype(jnp.float32)
+    return jnp.concatenate([high, value - high], axis=0).astype(jnp.bfloat16)
+
+
+def features_kernel(pieces, slot_count, tile_count, tile_side, map_ref, *refs):
+    piece_refs, out_ref, terms = refs[:pieces], refs[pieces], refs[pieces + 1]
+    grid = FaceStencil(tile_count, tile_side)
+    me = lax.axis_index("tile")
+    for piece in range(pieces):
+        for slot in range(slot_count):
+            place = map_ref[(me ^ piece) * slot_count + slot]
+            terms[0, place] = piece_refs[piece][slot].astype(jnp.float32)
+    for tile in range(tile_count):
+        out_ref[tile, 0:16] = split_rows(terms[0, tile])
+    for degree in range(1, K):
+        source = terms.at[degree - 1]
+        for tile in range(tile_count):
+            sums = grid.neighbour_sum(source, tile)
+            for number, total in enumerate(sums):
+                lanes = slice(number * LANES, (number + 1) * LANES)
+                if degree == 1:
+                    term = -0.25 * total
+                else:
+                    term = -0.5 * total - terms[degree - 2, tile, :, lanes]
+                terms[degree, tile, :, lanes] = term
+                out_ref[tile, 16 * degree : 16 * degree + 16, lanes] = split_rows(term)
+
+
+def gradient_kernel(
+    pieces, groups, slot_count, tile_count, tile_side, scale_factor, map_ref, *refs
+):
+    group_refs = refs[:groups]
+    terms_ref, filters_ref, in_grad_ref, weight_grad_ref = refs[groups : groups + 4]
+    whole, weights, mixed, sums_a, sums_b = refs[groups + 4 :]
+    grid = FaceStencil(tile_count, tile_side)
+    me = lax.axis_index("tile")
+    group = lax.axis_index("sub")
+    group_channels = group_refs[0].shape[1]
+    channels = groups * group_channels
+
+    for piece in range(pieces):
+        for slot in range(slot_count):
+            place = map_ref[(me ^ piece) * slot_count + slot]
+            rows = [
+                group_refs[other][piece * slot_count + slot].astype(jnp.float32)
+                for other in range(groups)
+            ]
+            whole[place] = jnp.concatenate(rows, axis=0).astype(jnp.bfloat16)
+
+    lane = lax.broadcasted_iota(jnp.int32, (1, LANES), 1)
+    order = jnp.where(lane < channels, lane ^ (group * group_channels), lane)
+    weights[...] = jnp.zeros_like(weights)
+    weights[:, :, 0:channels] = filters_ref[...].astype(jnp.float32)
+    first = pl.multiple_of(group * group_channels, group_channels)
+    rows = [
+        lane_gather(weights[degree, pl.ds(first, group_channels), :], order)[:, :channels]
+        for degree in range(K)
+    ]
+    row_block = jnp.concatenate(rows, axis=0).astype(jnp.bfloat16)
+
+    total = jnp.zeros((16 * K, channels), jnp.float32)
+    for tile in range(tile_count):
+        cotangent = whole[tile]
+        mixed[tile] = jnp.dot(row_block, cotangent, preferred_element_type=jnp.float32)
+        total = total + lax.dot_general(
+            terms_ref[tile],
+            cotangent,
+            (((1,), (1,)), ((), ())),
+            preferred_element_type=jnp.float32,
+        )
+    total = jnp.concatenate(
+        [total, jnp.zeros((16 * K, LANES - channels), jnp.float32)], axis=1
+    )
+    for degree in range(K):
+        high = total[16 * degree : 16 * degree + 8]
+        low = total[16 * degree + 8 : 16 * degree + 16]
+        part = lane_gather((high + low) * scale_factor, order)
+        weight_grad_ref[degree] = part[:, :channels]
+
+    def term(degree, tile, lanes):
+        first_row = degree * group_channels
+        return mixed[tile, first_row : first_row + group_channels, lanes]
+
+    whole_lanes = slice(0, tile_side * tile_side)
+    for tile in range(tile_count):
+        sums_a[tile] = term(K - 1, tile, whole_lanes)
+    current, other = sums_a, sums_b
+    for degree in range(K - 2, -1, -1):
+        for tile in range(tile_count):
+            sums = grid.neighbour_sum(current, tile)
+            for number, neighbours in enumerate(sums):
+                lanes = slice(number * LANES, (number + 1) * LANES)
+                factor = -0.5 if degree > 0 else -0.25
+                value = term(degree, tile, lanes) + factor * neighbours
+                if degree < K - 2:
+                    value = value - other[tile, :, lanes]
+                other[tile, :, lanes] = value
+        current, other = other, current
+    for slot in range(slot_count):
+        place = map_ref[me * slot_count + slot]
+        in_grad_ref[slot] = current[place].astype(jnp.bfloat16)
+
+
+def by_gathering(features, out_grad, filters, tile_map):
+    slot_count, group_channels, pixels = features.shape
+    tile_side = math.isqrt(pixels)
+    device_count = lax.axis_size("tile")
+    groups = lax.axis_size("sub")
+    tile_count = slot_count * device_count
+    scale_factor = 1.0 / math.sqrt(tile_count * pixels)
+
+    def exchanged(value, axis, distance):
+        count = lax.axis_size(axis)
+        return lax.ppermute(value, axis, [(index, index ^ distance) for index in range(count)])
+
+    order = range(device_count - 1, 0, -1)
+    cotangents = {0: out_grad}
+    for distance in order:
+        cotangents[distance] = exchanged(out_grad, "tile", distance)
+    inputs = {0: features}
+    for distance in order:
+        inputs[distance] = exchanged(features, "tile", distance)
+    stacked = jnp.concatenate([cotangents[piece] for piece in range(device_count)], axis=0)
+    by_group = {0: stacked}
+    distance = groups // 2
+    while distance:
+        for known in list(by_group):
+            by_group[known + distance] = exchanged(by_group[known], "sub", distance)
+        distance //= 2
+
+    in_smem = pl.BlockSpec(memory_space=pltpu.SMEM)
+    in_vmem = pl.BlockSpec(memory_space=pltpu.VMEM)
+    terms = pl.pallas_call(
+        functools.partial(features_kernel, device_count, slot_count, tile_count, tile_side),
+        out_shape=jax.ShapeDtypeStruct((tile_count, 16 * K, pixels), jnp.bfloat16),
+        in_specs=[in_smem] + [in_vmem] * device_count,
+        out_specs=in_vmem,
+        scratch_shapes=[pltpu.VMEM((K, tile_count, group_channels, pixels), jnp.float32)],
+        name="feature_terms",
+    )(tile_map, *[inputs[piece] for piece in range(device_count)])
+    field = (tile_count, group_channels, pixels)
+    return pl.pallas_call(
+        functools.partial(
+            gradient_kernel, device_count, groups, slot_count, tile_count, tile_side, scale_factor
+        ),
+        out_shape=(
+            jax.ShapeDtypeStruct(features.shape, jnp.bfloat16),
+            jax.ShapeDtypeStruct((K, group_channels, groups * group_channels), jnp.float32),
+        ),
+        in_specs=[in_smem] + [in_vmem] * (groups + 2),
+        out_specs=(in_vmem, in_vmem),
+        scratch_shapes=[
+            pltpu.VMEM((tile_count, groups * group_channels, pixels), jnp.bfloat16),
+            pltpu.VMEM((K, groups * group_channels, LANES), jnp.float32),
+            pltpu.VMEM((tile_count, K * group_channels, pixels), jnp.float32),
+            pltpu.VMEM(field, jnp.float32),
+            pltpu.VMEM(field, jnp.float32),
+        ],
+        name="gradients",
+    )(tile_map, *[by_group[other] for other in range(groups)], terms, filters)
+
+
+def on_device(features, out_grad, filters, tile_map):
+    slot_count, group_channels, pixels = features.shape
+    device_count = lax.axis_size("tile")
+    groups = lax.axis_size("sub")
+    tile_side = math.isqrt(pixels)
+    map_bytes = 2 * slot_count * device_count * groups * group_channels * pixels
+    fits = (
+        map_bytes <= GATHER_LIMIT
+        and group_channels == 8
+        and LANES % tile_side == 0
+        and pixels % LANES == 0
+        and device_count & (device_count - 1) == 0
+        and groups & (groups - 1) == 0
+        and groups * group_channels <= LANES
+    )
+    step = by_gathering if fits else by_halos
+    return step(features, out_grad, filters, tile_map)
+
+
 def solution(mesh):
     placed = (P(("grp", "tile"), "sub", None), P(("grp", "tile"), "sub", None), P(), P())
     return jax.shard_map(

time: 90.1 us -> 45.4 us (0.50)
  starting transfers between devices: 36.9 us -> 11.6 us
  blocking collectives: 23.9 us -> 0 us
  local copies, waits for them, and re-layouts: 22.3 us -> 2.82 us
  Pallas kernels: 0 us -> 17.5 us
  waiting for transfers between devices: 0.06 us -> 12.5 us
  matrix products: 2.63 us -> 0 us
  other arithmetic: 2.6 us -> 0 us
    ppermute x24 -> x9, starting transfers between devices: 36.9 us -> 11.6 us  [exchanged(): lax.ppermute(value, axis, [(index, index ^ distance) for index in range(c...]
    psum x1 -> x0, blocking collectives: 18.3 us -> none  [tile_total(): return lax.psum(filter_part, 'tile')]
    pallas_call x0 -> x2, Pallas kernels: none -> 17.5 us  [the longest x1 8.95 us: by_gathering(): pl.pallas_call(functools.partial(features_kernel, device_count, slot_coun...]
    ppermute x24 -> x9, waiting for transfers between devices: 0.06 us -> 12.5 us  [exchanged(): lax.ppermute(value, axis, [(index, index ^ distance) for index in range(c...]
    gather x11 -> x0, local copies, waits for them, and re-layouts: 6.38 us -> none  [the longest x8 4.87 us: laplace(): ghosts = stacked[local_rows, my_edges]]
    all_gather x1 -> x0, blocking collectives: 5.58 us -> none  [on_device(): whole_grad = lax.all_gather(out_grad, 'sub', axis=1, tiled=True)]
    slice x40 -> x0, local copies, waits for them, and re-layouts: 5.42 us -> none  [the longest x8 1.34 us: edge_lines(): values[..., -tile_side:]]
    reshape x24 -> x0, local copies, waits for them, and re-layouts: 3.72 us -> none  [the longest x8 1.41 us: stencil(): jnp.repeat(ghosts[:, 3], tile_side, axis=-1)]
  transfers between devices with their start and end apart: 24 -> 9, of which waited for: 0 -> 5; matrix products, arithmetic and copies ran while one was open for 26% -> 2% of each run, Pallas kernels for 0% -> 20%
where the time goes in v1:
time: 45.4 us; the launch traced here: 45.1 us
  Pallas kernels  17.5 us (39%)
  waiting for transfers between devices  12.5 us (28%)
  starting transfers between devices  11.6 us (26%)
  local copies, waits for them, and re-layouts  2.82 us (6%)
  between operations  0.68 us (1%)
    ppermute x9, waiting for transfers between devices, exchanged(): lax.ppermute(value, axis, [(index, index ^ distance) for index in range(c...  12.5 us
    ppermute x9, starting transfers between devices, exchanged(): lax.ppermute(value, axis, [(index, index ^ distance) for index in range(c...  11.6 us
    pallas_call x1, Pallas kernels, by_gathering(): pl.pallas_call(functools.partial(features_kernel, device_count, slot_coun...  8.95 us
    pallas_call x1, Pallas kernels, by_gathering(): pl.pallas_call(functools.partial(gradient_kernel, device_count, groups, s...  8.56 us
    unnamed x17, local copies, waits for them, and re-layouts  2.82 us
  transfers between devices with their start and end apart: 9, of which 5 were waited for; matrix products, arithmetic and copies ran while one was open for 2% of the time, Pallas kernels for 20%

profile of v1, /device:TPU:0, one launch (start us, length us, event | category | flops | bytes accessed | tf_op | source)
XLA Modules:
  0.0 45.1 jit_solution(7870398712695595761)
XLA Ops:
  0.6 4.1 %collective-permute-start.1 = (bf16[3,8,1024]{2,1,0:T(8,128)(2,1)}, bf16[3,8,1024]{2,1,0:T(8,128)(2,1)S(1)}, u32[]{:S(2)}, u32[]{:S(2)}) collective-permute-start(bf16[3,8,1024]{2,1,0:T(8,128)(2,1)} %param.5), channel_id=1, source_target_pairs={{0,8},{4,12},{8,0},{12,4},{1,9},{5,13},{9,1},{13,5},{2,10},{6,14},... | collective-permute-start | bytes 147464 | tf_op jit(solution)/shard_map/ppermute | solution.py:440
  4.8 1.6 %collective-permute-start = (bf16[3,8,1024]{2,1,0:T(8,128)(2,1)}, bf16[3,8,1024]{2,1,0:T(8,128)(2,1)S(1)}, u32[]{:S(2)}, u32[]{:S(2)}) collective-permute-start(bf16[3,8,1024]{2,1,0:T(8,128)(2,1)} %param.5), channel_id=1, source_target_pairs={{0,4},{4,0},{8,12},{12,8},{1,5},{5,1},{9,13},{13,9},{2,6},{6,2},{1... | collective-permute-start | bytes 147464 | tf_op jit(solution)/shard_map/ppermute | solution.py:440
  6.3 0.0 collective-permute-start.2
  6.3 0.9 %constant_dynamic-update-slice_fusion.3 = bf16[12,8,1024]{2,1,0:T(8,128)(2,1)S(1)} fusion(bf16[3,8,1024]{2,1,0:T(8,128)(2,1)} %param.5), kind=kLoop, calls=%fused_computation.3 | loop fusion | bytes 98304
  7.2 1.9 %collective-permute-done = bf16[3,8,1024]{2,1,0:T(8,128)(2,1)S(1)} collective-permute-done((bf16[3,8,1024]{2,1,0:T(8,128)(2,1)}, bf16[3,8,1024]{2,1,0:T(8,128)(2,1)S(1)}, u32[]{:S(2)}, u32[]{:S(2)}) %collective-permute-start) | collective-permute-done | bytes 49184 | tf_op jit(solution)/shard_map/ppermute | solution.py:440
  9.1 0.0 collective-permute-done.1
  9.1 3.4 %collective-permute-done.2 = bf16[3,8,1024]{2,1,0:T(8,128)(2,1)S(1)} collective-permute-done((bf16[3,8,1024]{2,1,0:T(8,128)(2,1)}, bf16[3,8,1024]{2,1,0:T(8,128)(2,1)S(1)}, u32[]{:S(2)}, u32[]{:S(2)}) %collective-permute-start.2) | collective-permute-done | bytes 49184 | tf_op jit(solution)/shard_map/ppermute | solution.py:440
  12.4 0.0 copy-start
  12.4 1.5 %collective-permute-start.4 = (bf16[12,8,1024]{2,1,0:T(8,128)(2,1)S(1)}, bf16[12,8,1024]{2,1,0:T(8,128)(2,1)S(1)}, u32[]{:S(2)}, u32[]{:S(2)}) collective-permute-start(bf16[12,8,1024]{2,1,0:T(8,128)(2,1)S(1)} %constant_dynamic-update-slice_fusion.refs_0_), channel_id=1, source_target_pairs={{0,2},{1,3},{2,0},{3,1},{4,6},{5,7},{6,4},{7,5},{8,10},{9,11},{10,... | collective-permute-start | bytes 589832 | tf_op jit(solution)/shard_map/ppermute | solution.py:440
  13.9 0.0 collective-permute-start.3
  13.9 4.2 %collective-permute-done.4.refs_2_ = bf16[12,8,1024]{2,1,0:T(8,128)(2,1)S(1)} collective-permute-done((bf16[12,8,1024]{2,1,0:T(8,128)(2,1)S(1)}, bf16[12,8,1024]{2,1,0:T(8,128)(2,1)S(1)}, u32[]{:S(2)}, u32[]{:S(2)}) %collective-permute-start.4) | collective-permute-done | bytes 196640 | tf_op jit(solution)/shard_map/ppermute | solution.py:440
  18.1 0.0 copy-start.1
  18.1 0.0 collective-permute-start.5
  18.1 0.1 collective-permute-start.7
  18.2 1.1 %collective-permute-start.6 = (bf16[3,8,1024]{2,1,0:T(8,128)(2,1)}, bf16[3,8,1024]{2,1,0:T(8,128)(2,1)S(1)}, u32[]{:S(2)}, u32[]{:S(2)}) collective-permute-start(bf16[3,8,1024]{2,1,0:T(8,128)(2,1)} %refs_0_.1), channel_id=1, source_target_pairs={{0,4},{4,0},{8,12},{12,8},{1,5},{5,1},{9,13},{13,9},{2,6},{6,2},{1... | collective-permute-start | bytes 147464 | tf_op jit(solution)/shard_map/ppermute | solution.py:440
  19.3 3.2 %collective-permute-start.8 = (bf16[3,8,1024]{2,1,0:T(8,128)(2,1)}, bf16[3,8,1024]{2,1,0:T(8,128)(2,1)S(1)}, u32[]{:S(2)}, u32[]{:S(2)}) collective-permute-start(bf16[3,8,1024]{2,1,0:T(8,128)(2,1)} %refs_0_.1), channel_id=1, source_target_pairs={{0,12},{4,8},{8,4},{12,0},{1,13},{5,9},{9,5},{13,1},{2,14},{6,10},... | collective-permute-start | bytes 147464 | tf_op jit(solution)/shard_map/ppermute | solution.py:440
  22.5 1.3 %collective-permute-done.7.refs_2_ = bf16[3,8,1024]{2,1,0:T(8,128)(2,1)S(1)} collective-permute-done((bf16[3,8,1024]{2,1,0:T(8,128)(2,1)}, bf16[3,8,1024]{2,1,0:T(8,128)(2,1)S(1)}, u32[]{:S(2)}, u32[]{:S(2)}) %collective-permute-start.7) | collective-permute-done | bytes 49184 | tf_op jit(solution)/shard_map/ppermute | solution.py:440
  23.8 0.0 copy-start.4
  23.8 0.0 collective-permute-done.6.refs_1_
  23.8 0.0 copy-start.5
  23.9 1.8 %collective-permute-done.8.refs_3_ = bf16[3,8,1024]{2,1,0:T(8,128)(2,1)S(1)} collective-permute-done((bf16[3,8,1024]{2,1,0:T(8,128)(2,1)}, bf16[3,8,1024]{2,1,0:T(8,128)(2,1)S(1)}, u32[]{:S(2)}, u32[]{:S(2)}) %collective-permute-start.8) | collective-permute-done | bytes 49184 | tf_op jit(solution)/shard_map/ppermute | solution.py:440
  25.6 0.0 copy-done.4
  25.6 0.0 copy-done.5
  25.6 0.0 copy-start.6
  25.6 0.6 %copy-done.6 = bf16[3,8,1024]{2,1,0:T(8,128)(2,1)} copy-done((bf16[3,8,1024]{2,1,0:T(8,128)(2,1)}, bf16[3,8,1024]{2,1,0:T(8,128)(2,1)S(1)}, u32[]{:S(2)}) %copy-start.6) | copy-done | bytes 49176
  26.2 8.9 %feature_terms.1.refs_4_ = bf16[12,80,1024]{2,1,0:T(8,128)(2,1)} custom-call(s32[12]{0:T(128)} %map_ref.3, bf16[3,8,1024]{2,1,0:T(8,128)(2,1)} %refs_0_.1, bf16[3,8,1024]{2,1,0:T(8,128)(2,1)} %copy-done.5, bf16[3,8,1024]{2,1,0:T(8,128)(2,1)} %copy-done.4, bf16[3,8,1024]{2,1,0:T(8,128)(2,1)} %copy-done.6), custom_call_target="tpu_custom_call" | custom-call | tf_op jit(solution)/shard_map/feature_terms/pallas_call | solution.py:459
  35.2 0.0 collective-permute-done.3.refs_1_
  35.2 0.0 copy-start.2
  35.2 0.0 collective-permute-done.5.refs_3_
  35.2 0.0 copy-done
  35.2 0.0 copy-done.1
  35.2 0.6 %copy-done.2 = bf16[12,8,1024]{2,1,0:T(8,128)(2,1)} copy-done((bf16[12,8,1024]{2,1,0:T(8,128)(2,1)}, bf16[12,8,1024]{2,1,0:T(8,128)(2,1)S(1)}, u32[]{:S(2)}) %copy-start.2) | copy-done | bytes 196632
  35.9 0.0 copy-start.3
  35.9 0.7 %copy-done.3 = bf16[12,8,1024]{2,1,0:T(8,128)(2,1)} copy-done((bf16[12,8,1024]{2,1,0:T(8,128)(2,1)}, bf16[12,8,1024]{2,1,0:T(8,128)(2,1)S(1)}, u32[]{:S(2)}) %copy-start.3) | copy-done | bytes 196632
  36.5 8.6 %gradients.1 = (bf16[3,8,1024]{2,1,0:T(8,128)(2,1)}, f32[5,8,32]{2,1,0:T(8,128)}) custom-call(s32[12]{0:T(128)} %map_ref.3, bf16[12,8,1024]{2,1,0:T(8,128)(2,1)} %copy-done, bf16[12,8,1024]{2,1,0:T(8,128)(2,1)} %copy-done.2, bf16[12,8,1024]{2,1,0:T(8,128)(2,1)} %copy-done.1, bf16[12,8,1024]{2,1,0:T(8,128)(2,1)} %copy-done.3, ...), custom_call_target="tpu_custom_call" | custom-call | tf_op jit(solution)/shard_map/gradients/pallas_call | solution.py:468
  (3 shorter events, 0.0 us)
Async XLA Ops:
  0.6 8.4 %collective-permute-start.1 = (bf16[3,8,1024]{2,1,0:T(8,128)(2,1)}, bf16[3,8,1024]{2,1,0:T(8,128)(2,1)S(1)}, u32[]{:S(2)}, u32[]{:S(2)}) collective-permute-start(bf16[3,8,1024]{2,1,0:T(8,128)(2,1)} %param.5), channel_id=1, source_target_pairs={{0,8},{4,12},{8,0},{12,4},{1,9},{5,13},{9,1},{13,5},{2,10},{6,14},... | collective-permute-start | bytes 147464 | tf_op jit(solution)/shard_map/ppermute | solution.py:440
  4.8 4.3 %collective-permute-start = (bf16[3,8,1024]{2,1,0:T(8,128)(2,1)}, bf16[3,8,1024]{2,1,0:T(8,128)(2,1)S(1)}, u32[]{:S(2)}, u32[]{:S(2)}) collective-permute-start(bf16[3,8,1024]{2,1,0:T(8,128)(2,1)} %param.5), channel_id=1, source_target_pairs={{0,4},{4,0},{8,12},{12,8},{1,5},{5,1},{9,13},{13,9},{2,6},{6,2},{1... | collective-permute-start | bytes 147464 | tf_op jit(solution)/shard_map/ppermute | solution.py:440
  6.3 6.1 %collective-permute-start.2 = (bf16[3,8,1024]{2,1,0:T(8,128)(2,1)}, bf16[3,8,1024]{2,1,0:T(8,128)(2,1)S(1)}, u32[]{:S(2)}, u32[]{:S(2)}) collective-permute-start(bf16[3,8,1024]{2,1,0:T(8,128)(2,1)} %param.5), channel_id=1, source_target_pairs={{0,12},{4,8},{8,4},{12,0},{1,13},{5,9},{9,5},{13,1},{2,14},{6,10},... | collective-permute-start | bytes 147464 | tf_op jit(solution)/shard_map/ppermute | solution.py:440
  12.4 22.8 %copy-start = (bf16[12,8,1024]{2,1,0:T(8,128)(2,1)}, bf16[12,8,1024]{2,1,0:T(8,128)(2,1)S(1)}, u32[]{:S(2)}) copy-start(bf16[12,8,1024]{2,1,0:T(8,128)(2,1)S(1)} %constant_dynamic-update-slice_fusion.refs_0_) | copy-start | bytes 589828
  12.4 5.7 %collective-permute-start.4 = (bf16[12,8,1024]{2,1,0:T(8,128)(2,1)S(1)}, bf16[12,8,1024]{2,1,0:T(8,128)(2,1)S(1)}, u32[]{:S(2)}, u32[]{:S(2)}) collective-permute-start(bf16[12,8,1024]{2,1,0:T(8,128)(2,1)S(1)} %constant_dynamic-update-slice_fusion.refs_0_), channel_id=1, source_target_pairs={{0,2},{1,3},{2,0},{3,1},{4,6},{5,7},{6,4},{7,5},{8,10},{9,11},{10,... | collective-permute-start | bytes 589832 | tf_op jit(solution)/shard_map/ppermute | solution.py:440
  13.9 21.2 %collective-permute-start.3 = (bf16[12,8,1024]{2,1,0:T(8,128)(2,1)S(1)}, bf16[12,8,1024]{2,1,0:T(8,128)(2,1)S(1)}, u32[]{:S(2)}, u32[]{:S(2)}) collective-permute-start(bf16[12,8,1024]{2,1,0:T(8,128)(2,1)S(1)} %constant_dynamic-update-slice_fusion.refs_0_), channel_id=1, source_target_pairs={{0,1},{1,0},{2,3},{3,2},{4,5},{5,4},{6,7},{7,6},{8,9},{9,8},{10,11... | collective-permute-start | bytes 589832 | tf_op jit(solution)/shard_map/ppermute | solution.py:440
  18.1 17.1 %copy-start.1 = (bf16[12,8,1024]{2,1,0:T(8,128)(2,1)}, bf16[12,8,1024]{2,1,0:T(8,128)(2,1)S(1)}, u32[]{:S(2)}) copy-start(bf16[12,8,1024]{2,1,0:T(8,128)(2,1)S(1)} %collective-permute-done.4.refs_2_) | copy-start | bytes 589828
  18.1 17.1 %collective-permute-start.5 = (bf16[12,8,1024]{2,1,0:T(8,128)(2,1)S(1)}, bf16[12,8,1024]{2,1,0:T(8,128)(2,1)S(1)}, u32[]{:S(2)}, u32[]{:S(2)}) collective-permute-start(bf16[12,8,1024]{2,1,0:T(8,128)(2,1)S(1)} %collective-permute-done.4.refs_2_), channel_id=1, source_target_pairs={{0,1},{1,0},{2,3},{3,2},{4,5},{5,4},{6,7},{7,6},{8,9},{9,8},{10,11... | collective-permute-start | bytes 589832 | tf_op jit(solution)/shard_map/ppermute | solution.py:440
  18.1 5.7 %collective-permute-start.7 = (bf16[3,8,1024]{2,1,0:T(8,128)(2,1)}, bf16[3,8,1024]{2,1,0:T(8,128)(2,1)S(1)}, u32[]{:S(2)}, u32[]{:S(2)}) collective-permute-start(bf16[3,8,1024]{2,1,0:T(8,128)(2,1)} %refs_0_.1), channel_id=1, source_target_pairs={{0,8},{4,12},{8,0},{12,4},{1,9},{5,13},{9,1},{13,5},{2,10},{6,14},... | collective-permute-start | bytes 147464 | tf_op jit(solution)/shard_map/ppermute | solution.py:440
  18.2 5.7 %collective-permute-start.6 = (bf16[3,8,1024]{2,1,0:T(8,128)(2,1)}, bf16[3,8,1024]{2,1,0:T(8,128)(2,1)S(1)}, u32[]{:S(2)}, u32[]{:S(2)}) collective-permute-start(bf16[3,8,1024]{2,1,0:T(8,128)(2,1)} %refs_0_.1), channel_id=1, source_target_pairs={{0,4},{4,0},{8,12},{12,8},{1,5},{5,1},{9,13},{13,9},{2,6},{6,2},{1... | collective-permute-start | bytes 147464 | tf_op jit(solution)/shard_map/ppermute | solution.py:440
  19.3 6.3 %collective-permute-start.8 = (bf16[3,8,1024]{2,1,0:T(8,128)(2,1)}, bf16[3,8,1024]{2,1,0:T(8,128)(2,1)S(1)}, u32[]{:S(2)}, u32[]{:S(2)}) collective-permute-start(bf16[3,8,1024]{2,1,0:T(8,128)(2,1)} %refs_0_.1), channel_id=1, source_target_pairs={{0,12},{4,8},{8,4},{12,0},{1,13},{5,9},{9,5},{13,1},{2,14},{6,10},... | collective-permute-start | bytes 147464 | tf_op jit(solution)/shard_map/ppermute | solution.py:440
  23.8 1.8 %copy-start.4 = (bf16[3,8,1024]{2,1,0:T(8,128)(2,1)}, bf16[3,8,1024]{2,1,0:T(8,128)(2,1)S(1)}, u32[]{:S(2)}) copy-start(bf16[3,8,1024]{2,1,0:T(8,128)(2,1)S(1)} %collective-permute-done.7.refs_2_) | copy-start | bytes 147460
  23.8 1.8 %copy-start.5 = (bf16[3,8,1024]{2,1,0:T(8,128)(2,1)}, bf16[3,8,1024]{2,1,0:T(8,128)(2,1)S(1)}, u32[]{:S(2)}) copy-start(bf16[3,8,1024]{2,1,0:T(8,128)(2,1)S(1)} %collective-permute-done.6.refs_1_) | copy-start | bytes 147460
  25.6 0.6 %copy-start.6 = (bf16[3,8,1024]{2,1,0:T(8,128)(2,1)}, bf16[3,8,1024]{2,1,0:T(8,128)(2,1)S(1)}, u32[]{:S(2)}) copy-start(bf16[3,8,1024]{2,1,0:T(8,128)(2,1)S(1)} %collective-permute-done.8.refs_3_) | copy-start | bytes 147460
  35.2 0.7 %copy-start.2 = (bf16[12,8,1024]{2,1,0:T(8,128)(2,1)}, bf16[12,8,1024]{2,1,0:T(8,128)(2,1)S(1)}, u32[]{:S(2)}) copy-start(bf16[12,8,1024]{2,1,0:T(8,128)(2,1)S(1)} %collective-permute-done.3.refs_1_) | copy-start | bytes 589828
  35.9 0.7 %copy-start.3 = (bf16[12,8,1024]{2,1,0:T(8,128)(2,1)}, bf16[12,8,1024]{2,1,0:T(8,128)(2,1)S(1)}, u32[]{:S(2)}) copy-start(bf16[12,8,1024]{2,1,0:T(8,128)(2,1)S(1)} %collective-permute-done.5.refs_3_) | copy-start | bytes 589828

commit v2 on v0

--- a/solution.py
+++ b/solution.py
@@ -1,10 +1,14 @@
+import functools
 import math
 
 import jax
 import jax.numpy as jnp
 import numpy as np
 from jax import lax
+from jax.experimental import pallas as pl
+from jax.experimental.pallas import tpu as pltpu
 from jax.sharding import PartitionSpec as P
+
 
 K = 5
 
@@ -111,7 +115,7 @@
 
 def peer_offsets(slot_count, device_count, per_face, side_count):
     tile_ids = np.arange(slot_count * device_count, dtype=np.int64)
-    target_list, edge_list = neighbour_codes(tile_ids, per_face, side_count)
+    target_list, _ = neighbour_codes(tile_ids, per_face, side_count)
     targets = np.stack(target_list, axis=1)
     offsets = (tile_ids[:, None] // slot_count - targets // slot_count) % device_count
     distinct = sorted(set((int(value) for value in offsets.ravel())) - {0})
@@ -155,7 +159,7 @@
     return lax.psum(filter_part, "tile")
 
 
-def on_device(features, out_grad, filters, tile_map):
+def by_halos(features, out_grad, filters, tile_map):
     slot_count = features.shape[0]
     group_channels = features.shape[1]
     tile_side = math.isqrt(features.shape[2])
@@ -193,7 +197,7 @@
         jnp.einsum("sip,sop->io", inputs, cotangent, precision=highest),
         jnp.einsum("sip,sop->io", current, cotangent, precision=highest),
     ]
-    for degree in range(2, K):
+    for _ in range(2, K):
         previous, current = (current, 2.0 * laplace(current) - previous)
         filter_terms.append(jnp.einsum("sip,sop->io", current, cotangent, precision=highest))
     weight_grad = tile_total(jnp.stack(filter_terms)) * scale_factor
@@ -208,6 +212,364 @@
         next_sum, after_next = (mixed(degree) + 2.0 * laplace(next_sum) - after_next, next_sum)
     in_grad = (mixed(0) + laplace(next_sum) - after_next).astype(jnp.bfloat16)
     return (in_grad, weight_grad)
+
+
+LANES = 128
+SUBLANES = 8
+GATHER_LIMIT = 2 << 20
+BLOCK = 256
+KERNEL_BYTES = 20 << 20
+
+
+def lane_iota(rows=1):
+    return lax.broadcasted_iota(jnp.int32, (rows, LANES), 1)
+
+
+def lane_gather(block, lane_index):
+    index = jnp.broadcast_to(lane_index, block.shape)
+    return jnp.take_along_axis(block, index, axis=1, mode="promise_in_bounds")
+
+
+def shuffled(value, lane_index):
+    parts = [
+        lane_gather(value[start : start + SUBLANES], lane_index)
+        for start in range(0, value.shape[0], SUBLANES)
+    ]
+    return jnp.concatenate(parts, axis=0)
+
+
+def identity(rows, columns):
+    shape = (rows, columns)
+    same = lax.broadcasted_iota(jnp.int32, shape, 0) == lax.broadcasted_iota(jnp.int32, shape, 1)
+    return same.astype(jnp.float32).astype(jnp.bfloat16)
+
+
+def product(left, right):
+    return jnp.dot(left, right, preferred_element_type=jnp.float32)
+
+
+def product_of_rows(left, right):
+    return lax.dot_general(
+        left, right, (((1,), (1,)), ((), ())), preferred_element_type=jnp.float32
+    )
+
+
+def high_and_low(value):
+    high = value.astype(jnp.bfloat16)
+    return high, (value - high.astype(jnp.float32)).astype(jnp.bfloat16)
+
+
+class Map:
+    def __init__(self, map_ref, slot_count, device_count, tile_side, channels):
+        self.side = tile_side
+        self.pixels = tile_side * tile_side
+        tile_count = slot_count * device_count
+        per_face = tile_count // 12
+        side_count = math.isqrt(per_face)
+        targets, edges = neighbour_codes(
+            np.arange(tile_count, dtype=np.int64), per_face, side_count
+        )
+        me = lax.axis_index("tile")
+        held = [
+            map_ref[(me ^ (place // slot_count)) * slot_count + place % slot_count]
+            for place in range(tile_count)
+        ]
+        lane = lane_iota()
+        channel = lane % channels
+        tile = jnp.full((1, LANES), -1, jnp.int32)
+        for place in range(tile_count):
+            tile = jnp.where(lane // channels == place, held[place], tile)
+        self.index = []
+        self.polar = []
+        for side in range(4):
+            regular = side ^ 1
+            target = jnp.full((1, LANES), -1, jnp.int32)
+            polar = jnp.zeros((1, LANES), jnp.int32)
+            for number in range(tile_count):
+                here = tile == number
+                target = jnp.where(here, int(targets[side][number]), target)
+                if int(edges[side][number]) != regular:
+                    polar = jnp.where(here, 1, polar)
+            index = lane
+            for place in range(tile_count):
+                index = jnp.where(target == held[place], channels * place + channel, index)
+            self.index.append(index)
+            self.polar.append(polar == 1)
+
+    def set_ghosts(self, field, left, right):
+        side, pixels = self.side, self.pixels
+        lines = [
+            field[side : 2 * side],
+            field[pixels : pixels + side],
+            field[pl.ds(side, side, stride=side)],
+            field[pl.ds(2 * side - 1, side, stride=side)],
+        ]
+
+        def ghost(which):
+            regular = shuffled(lines[which ^ 1], self.index[which])
+            turned = shuffled(lines[(2, 3, 0, 1)[which]], self.index[which])
+            return jnp.where(self.polar[which], turned, regular)
+
+        field[0:side] = ghost(0)
+        field[side + pixels : 2 * side + pixels] = ghost(1)
+        left[0:side] = ghost(2)
+        right[SUBLANES : SUBLANES + side] = ghost(3)
+
+    def neighbour_sum(self, field, left, right, start):
+        side = self.side
+        row, column = divmod(start, side)
+        base = side + start
+        sublane = lax.broadcasted_iota(jnp.int32, (SUBLANES, LANES), 0)
+
+        def rows(first):
+            return field[first : first + SUBLANES]
+
+        before, after = rows(base - 1), rows(base + 1)
+        if column == 0:
+            before = jnp.where(sublane == 0, left[row : row + SUBLANES], before)
+        if column == side - SUBLANES:
+            ghost = right[row + 1 : row + 1 + SUBLANES]
+            after = jnp.where(sublane == SUBLANES - 1, ghost, after)
+        return (rows(base - side) + rows(base + side)) + (before + after)
+
+
+def features_kernel(slot_count, device_count, tile_side, map_ref, *refs):
+    piece_refs, out_ref = refs[:device_count], refs[device_count]
+    fields, left, right = refs[device_count + 1 :]
+    channels = piece_refs[0].shape[1]
+    grid = Map(map_ref, slot_count, device_count, tile_side, channels)
+    side, pixels = tile_side, tile_side * tile_side
+    rows = [
+        piece_refs[piece][slot].astype(jnp.float32)
+        for piece in range(device_count)
+        for slot in range(slot_count)
+    ]
+    missing = LANES - channels * len(rows)
+    rows.append(jnp.zeros((missing, pixels), jnp.float32))
+    inputs = jnp.concatenate(rows, axis=0).astype(jnp.bfloat16)
+    one = identity(BLOCK, BLOCK)
+    for start in range(0, pixels, BLOCK):
+        value = product_of_rows(one, inputs[:, start : start + BLOCK])
+        fields[0, side + start : side + start + BLOCK] = value
+        out_ref[start : start + BLOCK, 0:LANES] = value.astype(jnp.bfloat16)
+    for degree in range(1, K):
+        source = fields.at[degree - 1]
+        grid.set_ghosts(source, left, right)
+        for start in range(0, pixels, 2 * SUBLANES):
+            pair = []
+            for first in (start, start + SUBLANES):
+                total = grid.neighbour_sum(source, left, right, first)
+                place = slice(side + first, side + first + SUBLANES)
+                if degree == 1:
+                    term = -0.25 * total
+                else:
+                    term = -0.5 * total - fields[degree - 2, place]
+                fields[degree, place] = term
+                pair.append(term)
+            high, low = high_and_low(jnp.concatenate(pair, axis=0))
+            place = slice(start, start + 2 * SUBLANES)
+            first_lane = (2 * degree - 1) * LANES
+            out_ref[place, first_lane : first_lane + LANES] = high
+            out_ref[place, first_lane + LANES : first_lane + 2 * LANES] = low
+
+
+def gradient_kernel(groups, slot_count, device_count, tile_side, scale_factor, map_ref, *refs):
+    group_refs = refs[:groups]
+    terms_ref, filters_ref, in_grad_ref, weight_grad_ref = refs[groups : groups + 4]
+    whole, spread, mixed, fields, left, right, products = refs[groups + 4 :]
+    group_channels = group_refs[0].shape[1]
+    channels = groups * group_channels
+    tile_count = slot_count * device_count
+    side, pixels = tile_side, tile_side * tile_side
+    grid = Map(map_ref, slot_count, device_count, tile_side, group_channels)
+    group = lax.axis_index("sub")
+    own = group * group_channels
+
+    shape = (channels, channels)
+    reorder = lax.broadcasted_iota(jnp.int32, shape, 1) == (
+        lax.broadcasted_iota(jnp.int32, shape, 0) ^ own
+    )
+    reorder = reorder.astype(jnp.float32).astype(jnp.bfloat16)
+    filter_rows = filters_ref[...].reshape(K * channels, channels)
+    turned = product_of_rows(reorder, filter_rows).astype(jnp.bfloat16)
+    shape = (K * channels, K * LANES)
+    row = lax.broadcasted_iota(jnp.int32, shape, 0)
+    lane = lax.broadcasted_iota(jnp.int32, shape, 1)
+    chosen = (row // channels == lane // LANES) & (
+        row % channels == own + lane % group_channels
+    )
+    repeated = product(turned, chosen.astype(jnp.float32).astype(jnp.bfloat16))
+    lane = lax.broadcasted_iota(jnp.int32, (1, K * LANES), 1)
+    for place in range(tile_count):
+        mine = lane % LANES // group_channels == place
+        spread[channels * place : channels * (place + 1)] = jnp.where(
+            mine, repeated, 0.0
+        ).astype(jnp.bfloat16)
+
+    for place in range(tile_count):
+        rows = [group_refs[other][place].astype(jnp.float32) for other in range(groups)]
+        whole[channels * place : channels * (place + 1)] = jnp.concatenate(rows, axis=0).astype(
+            jnp.bfloat16
+        )
+    one = identity(BLOCK, BLOCK)
+    for start in range(0, pixels, BLOCK):
+        turned = product_of_rows(one, whole[:, start : start + BLOCK]).astype(jnp.bfloat16)
+        value = product(turned, spread[...])
+        for degree in range(K - 1):
+            lanes = slice(LANES * degree, LANES * (degree + 1))
+            mixed[degree, start : start + BLOCK] = value[:, lanes]
+        fields[0, side + start : side + start + BLOCK] = value[:, LANES * (K - 1) :]
+
+    products[...] = product(whole[...], terms_ref[...])
+    lane = lane_iota()
+    sums = []
+    for degree in range(K):
+        total = jnp.zeros((channels, LANES), jnp.float32)
+        for place in range(tile_count):
+            rows = slice(channels * place, channels * (place + 1))
+            if degree == 0:
+                part = products[rows, 0:LANES]
+            else:
+                first_lane = (2 * degree - 1) * LANES
+                part = (
+                    products[rows, first_lane : first_lane + LANES]
+                    + products[rows, first_lane + LANES : first_lane + 2 * LANES]
+                )
+            total = total + jnp.where(lane // group_channels == place, part, 0.0)
+        distance = group_channels
+        while distance < LANES:
+            total = total + pltpu.roll(total, distance, 1)
+            distance *= 2
+        sums.append(total)
+    packed = sums[0]
+    for degree in range(1, K):
+        packed = jnp.where(lane // group_channels == degree, sums[degree], packed)
+    packed = jnp.concatenate(
+        [packed * scale_factor, jnp.zeros((LANES - channels, LANES), jnp.float32)], axis=0
+    )
+    turned = packed.T
+    order = jnp.where(lane < channels, lane ^ own, lane)
+    for degree in range(K):
+        rows = turned[group_channels * degree : group_channels * (degree + 1)]
+        weight_grad_ref[degree] = lane_gather(rows, order)[:, :channels]
+
+    current, other = 0, 1
+    for degree in range(K - 2, -1, -1):
+        source, result = fields.at[current], fields.at[other]
+        grid.set_ghosts(source, left, right)
+        factor = -0.5 if degree > 0 else -0.25
+        for start in range(0, pixels, SUBLANES):
+            total = grid.neighbour_sum(source, left, right, start)
+            value = mixed[degree, start : start + SUBLANES] + factor * total
+            place = slice(side + start, side + start + SUBLANES)
+            if degree < K - 2:
+                value = value - result[place]
+            result[place] = value
+        current, other = other, current
+    rows = slot_count * group_channels
+    rows += -rows % 16
+    pick_both = jnp.concatenate([identity(rows, LANES), identity(rows, LANES)], axis=1)
+    for start in range(0, pixels, BLOCK):
+        place = slice(side + start, side + start + BLOCK)
+        both = jnp.concatenate(high_and_low(fields[current, place]), axis=1)
+        value = product_of_rows(pick_both, both)
+        for slot in range(slot_count):
+            first_row = group_channels * slot
+            in_grad_ref[slot, :, start : start + BLOCK] = value[
+                first_row : first_row + group_channels
+            ].astype(jnp.bfloat16)
+
+
+def by_gathering(features, out_grad, filters, tile_map):
+    slot_count, group_channels, pixels = features.shape
+    tile_side = math.isqrt(pixels)
+    device_count = lax.axis_size("tile")
+    groups = lax.axis_size("sub")
+    tile_count = slot_count * device_count
+    channels = groups * group_channels
+    scale_factor = 1.0 / math.sqrt(tile_count * pixels)
+
+    def exchanged(value, axis, distance):
+        count = lax.axis_size(axis)
+        return lax.ppermute(
+            value, axis, [(index, index ^ distance) for index in range(count)]
+        )
+
+    order = range(device_count - 1, 0, -1)
+    cotangents = {0: out_grad}
+    for distance in order:
+        cotangents[distance] = exchanged(out_grad, "tile", distance)
+    inputs = {0: features}
+    for distance in order:
+        inputs[distance] = exchanged(features, "tile", distance)
+    stacked = jnp.concatenate([cotangents[piece] for piece in range(device_count)], axis=0)
+    by_group = {0: stacked}
+    distance = groups // 2
+    while distance:
+        for known in list(by_group):
+            by_group[known + distance] = exchanged(by_group[known], "sub", distance)
+        distance //= 2
+
+    in_smem = pl.BlockSpec(memory_space=pltpu.SMEM)
+    in_vmem = pl.BlockSpec(memory_space=pltpu.VMEM)
+    field = (pixels + 2 * tile_side, LANES)
+    beside = pltpu.VMEM((tile_side + SUBLANES, LANES), jnp.float32)
+    parts = 2 * K - 1
+    terms = pl.pallas_call(
+        functools.partial(features_kernel, slot_count, device_count, tile_side),
+        out_shape=jax.ShapeDtypeStruct((pixels, parts * LANES), jnp.bfloat16),
+        in_specs=[in_smem] + [in_vmem] * device_count,
+        out_specs=in_vmem,
+        scratch_shapes=[pltpu.VMEM((K,) + field, jnp.float32), beside, beside],
+        compiler_params=pltpu.CompilerParams(vmem_limit_bytes=KERNEL_BYTES),
+        cost_estimate=pl.CostEstimate(
+            flops=4 * 10**9, bytes_accessed=10**6, transcendentals=0
+        ),
+        name="feature_terms",
+    )(tile_map, *[inputs[piece] for piece in range(device_count)])
+    return pl.pallas_call(
+        functools.partial(
+            gradient_kernel, groups, slot_count, device_count, tile_side, scale_factor
+        ),
+        out_shape=(
+            jax.ShapeDtypeStruct(features.shape, jnp.bfloat16),
+            jax.ShapeDtypeStruct((K, group_channels, channels), jnp.float32),
+        ),
+        in_specs=[in_smem] + [in_vmem] * (groups + 2),
+        out_specs=(in_vmem, in_vmem),
+        scratch_shapes=[
+            pltpu.VMEM((tile_count * channels, pixels), jnp.bfloat16),
+            pltpu.VMEM((tile_count * channels, K * LANES), jnp.bfloat16),
+            pltpu.VMEM((K - 1, pixels, LANES), jnp.float32),
+            pltpu.VMEM((2,) + field, jnp.float32),
+            beside,
+            beside,
+            pltpu.VMEM((tile_count * channels, parts * LANES), jnp.float32),
+        ],
+        compiler_params=pltpu.CompilerParams(vmem_limit_bytes=KERNEL_BYTES),
+        name="gradients",
+    )(tile_map, *[by_group[other] for other in range(groups)], terms, filters)
+
+
+def on_device(features, out_grad, filters, tile_map):
+    slot_count, group_channels, pixels = features.shape
+    device_count = lax.axis_size("tile")
+    groups = lax.axis_size("sub")
+    tile_side = math.isqrt(pixels)
+    map_bytes = 2 * slot_count * device_count * groups * group_channels * pixels
+    fits = (
+        map_bytes <= GATHER_LIMIT
+        and group_channels == SUBLANES
+        and slot_count * device_count * group_channels < LANES
+        and K * group_channels <= LANES
+        and tile_side % 16 == 0
+        and pixels % BLOCK == 0
+        and device_count & (device_count - 1) == 0
+        and groups & (groups - 1) == 0
+        and groups * group_channels <= LANES
+    )
+    step = by_gathering if fits else by_halos
+    return step(features, out_grad, filters, tile_map)
 
 
 def solution(mesh):

time: 90.1 us -> 29.6 us (0.33)
  starting transfers between devices: 36.9 us -> 12.1 us
  blocking collectives: 23.9 us -> 0 us
  local copies, waits for them, and re-layouts: 22.3 us -> 2.34 us
  waiting for transfers between devices: 0.06 us -> 7.6 us
  Pallas kernels: 0 us -> 6.59 us
  matrix products: 2.63 us -> 0 us
  other arithmetic: 2.6 us -> 0 us
    ppermute x24 -> x9, starting transfers between devices: 36.9 us -> 12.1 us  [exchanged(): lax.ppermute(value, axis, [(index, index ^ distance) for index in range(c...]
    psum x1 -> x0, blocking collectives: 18.3 us -> none  [tile_total(): return lax.psum(filter_part, 'tile')]
    ppermute x24 -> x9, waiting for transfers between devices: 0.06 us -> 7.6 us  [exchanged(): lax.ppermute(value, axis, [(index, index ^ distance) for index in range(c...]
    pallas_call x0 -> x2, Pallas kernels: none -> 6.59 us  [the longest x1 4.83 us: by_gathering(): pl.pallas_call(functools.partial(gradient_kernel, groups, slot_count, dev...]
    gather x11 -> x0, local copies, waits for them, and re-layouts: 6.38 us -> none  [the longest x8 4.87 us: laplace(): ghosts = stacked[local_rows, my_edges]]
    all_gather x1 -> x0, blocking collectives: 5.58 us -> none  [on_device(): whole_grad = lax.all_gather(out_grad, 'sub', axis=1, tiled=True)]
    slice x40 -> x0, local copies, waits for them, and re-layouts: 5.42 us -> none  [the longest x8 1.34 us: edge_lines(): values[..., -tile_side:]]
    reshape x24 -> x0, local copies, waits for them, and re-layouts: 3.72 us -> none  [the longest x8 1.41 us: stencil(): jnp.repeat(ghosts[:, 3], tile_side, axis=-1)]
  transfers between devices with their start and end apart: 24 -> 9, of which waited for: 0 -> 5; matrix products, arithmetic and copies ran while one was open for 26% -> 3% of each run, Pallas kernels for 0% -> 6%
where the time goes in v2:
time: 29.6 us; the launch traced here: 29.3 us
  starting transfers between devices  12.1 us (41%)
  waiting for transfers between devices  7.6 us (26%)
  Pallas kernels  6.59 us (22%)
  local copies, waits for them, and re-layouts  2.34 us (8%)
  between operations  0.68 us (2%)
    ppermute x9, starting transfers between devices, exchanged(): lax.ppermute(value, axis, [(index, index ^ distance) for index in range(c...  12.1 us
    ppermute x9, waiting for transfers between devices, exchanged(): lax.ppermute(value, axis, [(index, index ^ distance) for index in range(c...  7.6 us
    pallas_call x1, Pallas kernels, by_gathering(): pl.pallas_call(functools.partial(gradient_kernel, groups, slot_count, dev...  4.83 us
    unnamed x9, local copies, waits for them, and re-layouts  2.33 us
    pallas_call x1, Pallas kernels, by_gathering(): pl.pallas_call(functools.partial(features_kernel, slot_count, device_coun...  1.77 us
  transfers between devices with their start and end apart: 9, of which 5 were waited for; matrix products, arithmetic and copies ran while one was open for 3% of the time, Pallas kernels for 6%

profile of v2, /device:TPU:0, one launch (start us, length us, event | category | flops | bytes accessed | tf_op | source)
XLA Modules:
  0.0 29.3 jit_solution(17178394831973707985)
XLA Ops:
  0.6 4.1 %collective-permute-start.1 = (bf16[3,8,1024]{2,1,0:T(8,128)(2,1)}, bf16[3,8,1024]{2,1,0:T(8,128)(2,1)S(1)}, u32[]{:S(2)}, u32[]{:S(2)}) collective-permute-start(bf16[3,8,1024]{2,1,0:T(8,128)(2,1)} %param.5), channel_id=1, source_target_pairs={{0,8},{4,12},{8,0},{12,4},{1,9},{5,13},{9,1},{13,5},{2,10},{6,14},... | collective-permute-start | bytes 147464 | tf_op jit(solution)/shard_map/ppermute | solution.py:494
  4.8 1.6 %collective-permute-start = (bf16[3,8,1024]{2,1,0:T(8,128)(2,1)}, bf16[3,8,1024]{2,1,0:T(8,128)(2,1)S(1)}, u32[]{:S(2)}, u32[]{:S(2)}) collective-permute-start(bf16[3,8,1024]{2,1,0:T(8,128)(2,1)} %param.5), channel_id=1, source_target_pairs={{0,4},{4,0},{8,12},{12,8},{1,5},{5,1},{9,13},{13,9},{2,6},{6,2},{1... | collective-permute-start | bytes 147464 | tf_op jit(solution)/shard_map/ppermute | solution.py:494
  6.3 0.0 collective-permute-start.2
  6.3 0.9 %constant_dynamic-update-slice_fusion.3 = bf16[12,8,1024]{2,1,0:T(8,128)(2,1)S(1)} fusion(bf16[3,8,1024]{2,1,0:T(8,128)(2,1)} %param.5), kind=kLoop, calls=%fused_computation.3 | loop fusion | bytes 98304
  7.2 1.9 %collective-permute-done = bf16[3,8,1024]{2,1,0:T(8,128)(2,1)S(1)} collective-permute-done((bf16[3,8,1024]{2,1,0:T(8,128)(2,1)}, bf16[3,8,1024]{2,1,0:T(8,128)(2,1)S(1)}, u32[]{:S(2)}, u32[]{:S(2)}) %collective-permute-start) | collective-permute-done | bytes 49184 | tf_op jit(solution)/shard_map/ppermute | solution.py:494
  9.1 0.0 collective-permute-done.1
  9.1 3.4 %collective-permute-done.2 = bf16[3,8,1024]{2,1,0:T(8,128)(2,1)S(1)} collective-permute-done((bf16[3,8,1024]{2,1,0:T(8,128)(2,1)}, bf16[3,8,1024]{2,1,0:T(8,128)(2,1)S(1)}, u32[]{:S(2)}, u32[]{:S(2)}) %collective-permute-start.2) | collective-permute-done | bytes 49184 | tf_op jit(solution)/shard_map/ppermute | solution.py:494
  12.4 0.0 copy-start
  12.4 1.5 %collective-permute-start.4 = (bf16[12,8,1024]{2,1,0:T(8,128)(2,1)S(1)}, bf16[12,8,1024]{2,1,0:T(8,128)(2,1)S(1)}, u32[]{:S(2)}, u32[]{:S(2)}) collective-permute-start(bf16[12,8,1024]{2,1,0:T(8,128)(2,1)S(1)} %constant_dynamic-update-slice_fusion.refs_0_), channel_id=1, source_target_pairs={{0,2},{1,3},{2,0},{3,1},{4,6},{5,7},{6,4},{7,5},{8,10},{9,11},{10,... | collective-permute-start | bytes 589832 | tf_op jit(solution)/shard_map/ppermute | solution.py:494
  13.9 0.1 collective-permute-start.7
  14.0 1.1 %collective-permute-start.6 = (bf16[3,8,1024]{2,1,0:T(8,128)(2,1)}, bf16[3,8,1024]{2,1,0:T(8,128)(2,1)S(1)}, u32[]{:S(2)}, u32[]{:S(2)}) collective-permute-start(bf16[3,8,1024]{2,1,0:T(8,128)(2,1)} %refs_0_.1), channel_id=1, source_target_pairs={{0,4},{4,0},{8,12},{12,8},{1,5},{5,1},{9,13},{13,9},{2,6},{6,2},{1... | collective-permute-start | bytes 147464 | tf_op jit(solution)/shard_map/ppermute | solution.py:494
  15.1 3.2 %collective-permute-start.8 = (bf16[3,8,1024]{2,1,0:T(8,128)(2,1)}, bf16[3,8,1024]{2,1,0:T(8,128)(2,1)S(1)}, u32[]{:S(2)}, u32[]{:S(2)}) collective-permute-start(bf16[3,8,1024]{2,1,0:T(8,128)(2,1)} %refs_0_.1), channel_id=1, source_target_pairs={{0,12},{4,8},{8,4},{12,0},{1,13},{5,9},{9,5},{13,1},{2,14},{6,10},... | collective-permute-start | bytes 147464 | tf_op jit(solution)/shard_map/ppermute | solution.py:494
  18.3 0.0 collective-permute-start.3
  18.3 0.0 collective-permute-done.4.refs_2_
  18.3 0.5 %collective-permute-start.5 = (bf16[12,8,1024]{2,1,0:T(8,128)(2,1)S(1)}, bf16[12,8,1024]{2,1,0:T(8,128)(2,1)S(1)}, u32[]{:S(2)}, u32[]{:S(2)}) collective-permute-start(bf16[12,8,1024]{2,1,0:T(8,128)(2,1)S(1)} %collective-permute-done.4.refs_2_), channel_id=1, source_target_pairs={{0,1},{1,0},{2,3},{3,2},{4,5},{5,4},{6,7},{7,6},{8,9},{9,8},{10,11... | collective-permute-start | bytes 589832 | tf_op jit(solution)/shard_map/ppermute | solution.py:494
  18.8 0.3 %collective-permute-done.7.refs_2_ = bf16[3,8,1024]{2,1,0:T(8,128)(2,1)S(1)} collective-permute-done((bf16[3,8,1024]{2,1,0:T(8,128)(2,1)}, bf16[3,8,1024]{2,1,0:T(8,128)(2,1)S(1)}, u32[]{:S(2)}, u32[]{:S(2)}) %collective-permute-start.7) | collective-permute-done | bytes 49184 | tf_op jit(solution)/shard_map/ppermute | solution.py:494
  19.1 0.1 collective-permute-done.6.refs_1_
  19.3 2.0 %collective-permute-done.8.refs_3_ = bf16[3,8,1024]{2,1,0:T(8,128)(2,1)S(1)} collective-permute-done((bf16[3,8,1024]{2,1,0:T(8,128)(2,1)}, bf16[3,8,1024]{2,1,0:T(8,128)(2,1)S(1)}, u32[]{:S(2)}, u32[]{:S(2)}) %collective-permute-start.8) | collective-permute-done | bytes 49184 | tf_op jit(solution)/shard_map/ppermute | solution.py:494
  21.2 0.0 copy-start.1
  21.2 0.7 %copy-done.1 = s32[12]{0:T(128)S(1)} copy-done((s32[12]{0:T(128)S(1)}, s32[12]{0:T(128)}, u32[]{:S(2)}) %copy-start.1) | copy-done | bytes 72
  21.9 0.0 copy-start.2
  21.9 0.8 %copy-done.2 = bf16[3,8,1024]{2,1,0:T(8,128)(2,1)S(1)} copy-done((bf16[3,8,1024]{2,1,0:T(8,128)(2,1)S(1)}, bf16[3,8,1024]{2,1,0:T(8,128)(2,1)}, u32[]{:S(2)}) %copy-start.2) | copy-done | bytes 49176
  22.7 1.8 %feature_terms.1.refs_4_ = bf16[1024,1152]{1,0:T(8,128)(2,1)S(1)} custom-call(s32[12]{0:T(128)S(1)} %copy-done.1, bf16[3,8,1024]{2,1,0:T(8,128)(2,1)S(1)} %copy-done.2, bf16[3,8,1024]{2,1,0:T(8,128)(2,1)S(1)} %collective-permute-done.6.refs_1_, bf16[3,8,1024]{2,1,0:T(8,128)(2,1)S(1)} %collective-permute-done.7.refs_2_, ...), custom_call_target="tpu_custom_call" | custom-call | flops 4000000000 | bytes 1000000 | tf_op jit(solution)/shard_map/feature_terms/pallas_call | solution.py:518
  24.5 0.0 collective-permute-done.3.refs_1_
  24.5 0.0 collective-permute-done.5.refs_3_
  24.5 0.0 copy-done
  24.5 4.8 %gradients.1 = (bf16[3,8,1024]{2,1,0:T(8,128)(2,1)}, f32[5,8,32]{2,1,0:T(8,128)}) custom-call(s32[12]{0:T(128)S(1)} %copy-done.1, bf16[12,8,1024]{2,1,0:T(8,128)(2,1)S(1)} %constant_dynamic-update-slice_fusion.refs_0_, bf16[12,8,1024]{2,1,0:T(8,128)(2,1)S(1)} %collective-permute-done.3.refs_1_, bf16[12,8,1024]{2,1,0:T(8,128)(2,1)S(1)} %collective-permute-done.4.refs_2_, ...), custom_call_target="tpu_custom_call" | custom-call | tf_op jit(solution)/shard_map/gradients/pallas_call | solution.py:530
  (3 shorter events, 0.0 us)
Async XLA Ops:
  0.6 8.4 %collective-permute-start.1 = (bf16[3,8,1024]{2,1,0:T(8,128)(2,1)}, bf16[3,8,1024]{2,1,0:T(8,128)(2,1)S(1)}, u32[]{:S(2)}, u32[]{:S(2)}) collective-permute-start(bf16[3,8,1024]{2,1,0:T(8,128)(2,1)} %param.5), channel_id=1, source_target_pairs={{0,8},{4,12},{8,0},{12,4},{1,9},{5,13},{9,1},{13,5},{2,10},{6,14},... | collective-permute-start | bytes 147464 | tf_op jit(solution)/shard_map/ppermute | solution.py:494
  4.8 4.3 %collective-permute-start = (bf16[3,8,1024]{2,1,0:T(8,128)(2,1)}, bf16[3,8,1024]{2,1,0:T(8,128)(2,1)S(1)}, u32[]{:S(2)}, u32[]{:S(2)}) collective-permute-start(bf16[3,8,1024]{2,1,0:T(8,128)(2,1)} %param.5), channel_id=1, source_target_pairs={{0,4},{4,0},{8,12},{12,8},{1,5},{5,1},{9,13},{13,9},{2,6},{6,2},{1... | collective-permute-start | bytes 147464 | tf_op jit(solution)/shard_map/ppermute | solution.py:494
  6.3 6.1 %collective-permute-start.2 = (bf16[3,8,1024]{2,1,0:T(8,128)(2,1)}, bf16[3,8,1024]{2,1,0:T(8,128)(2,1)S(1)}, u32[]{:S(2)}, u32[]{:S(2)}) collective-permute-start(bf16[3,8,1024]{2,1,0:T(8,128)(2,1)} %param.5), channel_id=1, source_target_pairs={{0,12},{4,8},{8,4},{12,0},{1,13},{5,9},{9,5},{13,1},{2,14},{6,10},... | collective-permute-start | bytes 147464 | tf_op jit(solution)/shard_map/ppermute | solution.py:494
  12.4 12.0 %copy-start = (bf16[5,32,32]{2,1,0:T(8,128)(2,1)S(1)}, bf16[5,32,32]{2,1,0:T(8,128)(2,1)}, u32[]{:S(2)}) copy-start(bf16[5,32,32]{2,1,0:T(8,128)(2,1)} %refs_5_.1) | copy-start | bytes 30724
  12.4 5.9 %collective-permute-start.4 = (bf16[12,8,1024]{2,1,0:T(8,128)(2,1)S(1)}, bf16[12,8,1024]{2,1,0:T(8,128)(2,1)S(1)}, u32[]{:S(2)}, u32[]{:S(2)}) collective-permute-start(bf16[12,8,1024]{2,1,0:T(8,128)(2,1)S(1)} %constant_dynamic-update-slice_fusion.refs_0_), channel_id=1, source_target_pairs={{0,2},{1,3},{2,0},{3,1},{4,6},{5,7},{6,4},{7,5},{8,10},{9,11},{10,... | collective-permute-start | bytes 589832 | tf_op jit(solution)/shard_map/ppermute | solution.py:494
  13.9 5.2 %collective-permute-start.7 = (bf16[3,8,1024]{2,1,0:T(8,128)(2,1)}, bf16[3,8,1024]{2,1,0:T(8,128)(2,1)S(1)}, u32[]{:S(2)}, u32[]{:S(2)}) collective-permute-start(bf16[3,8,1024]{2,1,0:T(8,128)(2,1)} %refs_0_.1), channel_id=1, source_target_pairs={{0,8},{4,12},{8,0},{12,4},{1,9},{5,13},{9,1},{13,5},{2,10},{6,14},... | collective-permute-start | bytes 147464 | tf_op jit(solution)/shard_map/ppermute | solution.py:494
  14.0 5.2 %collective-permute-start.6 = (bf16[3,8,1024]{2,1,0:T(8,128)(2,1)}, bf16[3,8,1024]{2,1,0:T(8,128)(2,1)S(1)}, u32[]{:S(2)}, u32[]{:S(2)}) collective-permute-start(bf16[3,8,1024]{2,1,0:T(8,128)(2,1)} %refs_0_.1), channel_id=1, source_target_pairs={{0,4},{4,0},{8,12},{12,8},{1,5},{5,1},{9,13},{13,9},{2,6},{6,2},{1... | collective-permute-start | bytes 147464 | tf_op jit(solution)/shard_map/ppermute | solution.py:494
  15.1 6.1 %collective-permute-start.8 = (bf16[3,8,1024]{2,1,0:T(8,128)(2,1)}, bf16[3,8,1024]{2,1,0:T(8,128)(2,1)S(1)}, u32[]{:S(2)}, u32[]{:S(2)}) collective-permute-start(bf16[3,8,1024]{2,1,0:T(8,128)(2,1)} %refs_0_.1), channel_id=1, source_target_pairs={{0,12},{4,8},{8,4},{12,0},{1,13},{5,9},{9,5},{13,1},{2,14},{6,10},... | collective-permute-start | bytes 147464 | tf_op jit(solution)/shard_map/ppermute | solution.py:494
  18.3 6.1 %collective-permute-start.3 = (bf16[12,8,1024]{2,1,0:T(8,128)(2,1)S(1)}, bf16[12,8,1024]{2,1,0:T(8,128)(2,1)S(1)}, u32[]{:S(2)}, u32[]{:S(2)}) collective-permute-start(bf16[12,8,1024]{2,1,0:T(8,128)(2,1)S(1)} %constant_dynamic-update-slice_fusion.refs_0_), channel_id=1, source_target_pairs={{0,1},{1,0},{2,3},{3,2},{4,5},{5,4},{6,7},{7,6},{8,9},{9,8},{10,11... | collective-permute-start | bytes 589832 | tf_op jit(solution)/shard_map/ppermute | solution.py:494
  18.3 6.1 %collective-permute-start.5 = (bf16[12,8,1024]{2,1,0:T(8,128)(2,1)S(1)}, bf16[12,8,1024]{2,1,0:T(8,128)(2,1)S(1)}, u32[]{:S(2)}, u32[]{:S(2)}) collective-permute-start(bf16[12,8,1024]{2,1,0:T(8,128)(2,1)S(1)} %collective-permute-done.4.refs_2_), channel_id=1, source_target_pairs={{0,1},{1,0},{2,3},{3,2},{4,5},{5,4},{6,7},{7,6},{8,9},{9,8},{10,11... | collective-permute-start | bytes 589832 | tf_op jit(solution)/shard_map/ppermute | solution.py:494
  21.2 0.7 %copy-start.1 = (s32[12]{0:T(128)S(1)}, s32[12]{0:T(128)}, u32[]{:S(2)}) copy-start(s32[12]{0:T(128)} %map_ref.3) | copy-start | bytes 148
  21.9 0.8 %copy-start.2 = (bf16[3,8,1024]{2,1,0:T(8,128)(2,1)S(1)}, bf16[3,8,1024]{2,1,0:T(8,128)(2,1)}, u32[]{:S(2)}) copy-start(bf16[3,8,1024]{2,1,0:T(8,128)(2,1)} %refs_0_.1) | copy-start | bytes 147460
